TPU v7x, 32 devices: a whole 2x2x4 slice. The times are simulated.
32 devices in a mesh: px: 8 (over z, y), py: 4 (over x, core).
Axes of the slice: x: 2, y: 2, z: 4, core: 2. Of those that a mesh axis runs over, the one named last changes fastest.
Arguments:
- flow_state: float32 [5, 64, 8, 32, 128], P(None, None, 'px', 'py'), may hold values from -1 to 3.2, as said below
- adjoint: float32 [5, 64, 8, 32, 128], P(None, None, 'px', 'py'), may hold values from -6 to 6
- displacement: float32 [3, 16, 36, 128], P(None, 'px', 'py'), may hold values from -0.1 to 0.1, as said below
- lattice_block: int32 [8, 4, 1024, 1], P('px', 'py'), may hold values from 0 to 31; in each aligned block of 1024 rows (0 to 1023, 1024 to 2047, ..., all dimensions but the last counted through in order) at most 64 rows name the same one
- lattice_coords: float32 [8, 4, 3, 1024], P('px', 'py'), may hold values from 0.02 to 0.98
Outputs:
- adjoint_residual: float32 [5, 64, 8, 32, 128], P(None, None, 'px', 'py')
- owned_vertex_sensitivity: float32 [3, 8, 32, 128], P(None, 'px', 'py')
- lattice_grad: float32 [8, 4, 3, 864], P('px', 'py')
Inputs may be any that keep to these rules, and one draw needn't show every extreme that they name: `flow_state`: field 0 (density) lies in 0.8 to 1.25, fields 1 to 3 (momenta) in -1 to 1, field 4 (energy) in 2 to 3.2. `displacement`: each device stores the vertex layers at both ends of its block along the first two dimensions; a vertex stored by two devices has equal values in both copies. `lattice_block`: among the 1024 vertices of one device no lattice block is named more than 64 times, and in some devices one block is named exactly 64 times.
All inputs are finite; a program needn't handle non-finite values.
Results may differ from a plain program's by a relative error of at most 0.0003.
Values sent between devices are 32-bit elements; how exact they have to be, the bound alone decides.
No kernel may reach another device: no remote copies, remote signals or barrier semaphores. Data moves between devices by JAX's collectives and lax.ppermute only.
A program may use at most 128 MiB of HBM per device.

v0:
```python
import functools
import math

import jax
import jax.numpy as jnp
import numpy as np
from jax import lax
from jax.experimental import pallas as pl
from jax.experimental.pallas import tpu as pltpu
from jax.sharding import PartitionSpec as P

LU = 12
LV = 12
LW = 6
HIGHEST = lax.Precision.HIGHEST
F32 = jnp.float32
POINTS = [-1.0, -1.0 / math.sqrt(5.0), 1.0 / math.sqrt(5.0), 1.0]
WEIGHTS = [1.0 / 6.0, 5.0 / 6.0, 5.0 / 6.0, 1.0 / 6.0]
UPPER = [0.5 * (1.0 + point) for point in POINTS]


def derivative_matrix():
    matrix = np.zeros((4, 4))
    for target in range(4):
        for source in range(4):
            others = [m for m in range(4) if m != source]
            if target == source:
                matrix[target, source] = sum(1.0 / (POINTS[source] - POINTS[m]) for m in others)
            else:
                upper = np.prod([POINTS[target] - POINTS[m] for m in others if m != target])
                lower = np.prod([POINTS[source] - POINTS[m] for m in others])
                matrix[target, source] = upper / lower
    return matrix


DM = derivative_matrix()


def line_slopes(line, scale):
    e0 = line[0] + line[3]
    o0 = line[0] - line[3]
    e1 = line[1] + line[2]
    o1 = line[1] - line[2]
    even = e0 - e1
    out = [None] * 4
    for m in range(2):
        half = 0.5 * scale[m]
        p0 = float(half * (DM[m, 0] - DM[m, 3]))
        p1 = float(half * (DM[m, 1] - DM[m, 2]))
        k = float(half * (DM[m, 0] + DM[m, 3]))
        odd_part = p0 * o0 + p1 * o1
        even_part = k * even
        out[m] = odd_part + even_part
        out[3 - m] = odd_part - even_part
    return out


def spread(low, high):
    step = high - low
    return [low, low + float(UPPER[1]) * step, low + float(UPPER[2]) * step, high]


def gather_back(g):
    middle = float(UPPER[1]) * g[1] + float(UPPER[2]) * g[2]
    return (g[0] + g[1] + g[2] - middle, g[3] + middle)


def cross(x, y):
    return [x[1] * y[2] - x[2] * y[1], x[2] * y[0] - x[0] * y[2], x[0] * y[1] - x[1] * y[0]]


def dot3(x, y):
    return x[0] * y[0] + x[1] * y[1] + x[2] * y[2]


def add(x, y):
    return y if x is None else x + y


def add3(x, y):
    return y if x is None else [x[i] + y[i] for i in range(3)]


def primitives(u):
    inverse = 1.0 / u[0]
    v = [u[1] * inverse, u[2] * inverse, u[3] * inverse]
    mv = u[1] * v[0] + u[2] * v[1] + u[3] * v[2]
    p = 0.4 * u[4] - 0.2 * mv
    return inverse, v, mv * inverse, p, u[4] + p


class Node:
    def __init__(self, u):
        self.inverse, self.v, self.v2, self.p, self.ep = primitives(u)
        self.big = [u[0], u[1], u[2], u[3], self.ep]
        self.w = [None] * 5
        self.pb = None
        self.b = None

    def work(self, s):
        return sum((s[f] * self.big[f] for f in range(1, 5)), s[0] * self.big[0])

    def volume(self, adj, s, vn):
        back = []
        for d in range(3):
            k = self.work(s[d])
            for f in range(5):
                self.w[f] = add(self.w[f], vn[d] * s[d][f])
            self.pb = add(self.pb, dot3(adj[d], s[d][1:4]))
            self.b = add3(self.b, [adj[d][c] * k for c in range(3)])
            back.append([self.v[c] * k + self.p * s[d][1 + c] for c in range(3)])
        self.pb = self.pb + self.w[4]
        return back

    def face(self, n, vn, jump, sigma):
        k = self.work(jump)
        square = dot3(n, n)
        root = lax.rsqrt(square)
        twice = 2.0 * root
        length = twice * square
        if isinstance(sigma, int) and sigma == 1:
            cf = vn + length
        elif isinstance(sigma, int):
            cf = vn - length
            twice = -twice
        else:
            cf = vn + sigma * length
            twice = sigma * twice
        q = k - jump[4] * self.p
        along = twice * q
        for f in range(5):
            self.w[f] = add(self.w[f], cf * jump[f])
        self.pb = add(self.pb, dot3(n, jump[1:4]) + vn * jump[4])
        self.b = add3(self.b, [n[c] * k for c in range(3)])
        return [self.v[c] * k + self.p * jump[1 + c] + n[c] * along for c in range(3)]

    def gradient(self):
        pb4 = 0.4 * self.pb
        rb = [self.b[c] * self.inverse for c in range(3)]
        out = [self.w[0] - dot3(self.v, rb) + (0.5 * pb4) * self.v2]
        for c in range(3):
            out.append(self.w[1 + c] + rb[c] - pb4 * self.v[c])
        out.append(self.w[4] + pb4)
        return out


def corner(disp_ref, c, e1, e2, e3):
    window = disp_ref[c, e1, e2 : e2 + 8, :]
    return pltpu.roll(window, 127, 1) if e3 else window


def volume_kernel(u_ref, lam_ref, disp_ref, yup_ref, ydn_ref, grad_ref, g_ref, j0t, j1t, j2t, j0b, j1b, j2b, s1, s2, yj):
    a = pl.program_id(0)

    @pl.when(a == 0)
    def _():
        for c in range(3):
            x = [[[corner(disp_ref, c, e1, e2, e3) for e3 in range(2)] for e2 in range(2)] for e1 in range(2)]
            for d in range(3):
                ends = []
                for i in range(2):
                    pair = []
                    for j in range(2):
                        low = [(0, i, j), (i, 0, j), (i, j, 0)][d]
                        high = [(1, i, j), (i, 1, j), (i, j, 1)][d]
                        half = 0.5 * (x[high[0]][high[1]][high[2]] - x[low[0]][low[1]][low[2]])
                        pair.append(half + 0.5 if c == d else half)
                    ends.append(spread(pair[0], pair[1]))
                for j in range(4):
                    values = spread(ends[0][j], ends[1][j])
                    for i in range(4):
                        [j0t, j1t, j2t][d][i, j, c] = values[i]
        j0b[...] = jnp.zeros_like(j0b)
        for f in range(5):
            for b in range(4):
                for c in range(4):
                    weight = -WEIGHTS[b] * WEIGHTS[c]
                    line = [lam_ref[f, 16 * i + 4 * b + c] for i in range(4)]
                    out = line_slopes(line, [weight] * 4)
                    for i in range(4):
                        s1[i, 4 * b + c, f] = out[i]

    wa = jnp.where((a == 0) | (a == 3), F32(WEIGHTS[0]), F32(WEIGHTS[1]))
    rows = lax.broadcasted_iota(jnp.int32, (8, 128), 0)
    first_row = rows == 0
    last_row = rows == 7
    base = a * 16
    for f in range(5):
        for c in range(4):
            line = [lam_ref[f, base + 4 * b + c] for b in range(4)]
            out = line_slopes(line, [-WEIGHTS[b] * WEIGHTS[c] for b in range(4)])
            for b in range(4):
                s2[4 * b + c, f] = out[b]
            half = float(0.5 * WEIGHTS[c])
            above = yup_ref[pl.ds(f * 16 + a * 4 + c, 1), :]
            below = ydn_ref[pl.ds(f * 16 + a * 4 + c, 1), :]
            plus = jnp.where(last_row, jnp.broadcast_to(above, (8, 128)), pltpu.roll(line[0], 7, 0))
            top = half * (line[3] - plus)
            bottom = half * (jnp.broadcast_to(below, (8, 128)) - line[0])
            yj[1, c, f] = top
            yj[0, c, f] = jnp.where(first_row, bottom, pltpu.roll(top, 1, 0))

    for b in range(4):
        slopes3 = []
        ztop = []
        zbot = []
        half = float(0.5 * WEIGHTS[b])
        for f in range(5):
            line = [lam_ref[f, base + 4 * b + c] for c in range(4)]
            slopes3.append(line_slopes(line, [-WEIGHTS[b] * WEIGHTS[c] for c in range(4)]))
            top = half * (line[3] - pltpu.roll(line[0], 127, 1))
            ztop.append(top)
            zbot.append(pltpu.roll(top, 1, 1))
        back2 = None
        col2 = [j2t[a, b, k] for k in range(3)]
        for c in range(4):
            n = 4 * b + c
            node = Node([u_ref[f, n] for f in range(5)])
            col0 = [j0t[b, c, k] for k in range(3)]
            col1 = [j1t[a, c, k] for k in range(3)]
            adj = [cross(col1, col2), cross(col2, col0), cross(col0, col1)]
            s = [[s1[a, n, f] for f in range(5)], [s2[n, f] for f in range(5)], [slopes3[f][c] for f in range(5)]]
            vn = [dot3(adj[d], node.v) for d in range(3)]
            back = node.volume(adj, s, vn)
            if b == 0:
                back[1] = add3(back[1], node.face(adj[1], vn[1], [yj[0, c, f] for f in range(5)], -1))
            if b == 3:
                back[1] = add3(back[1], node.face(adj[1], vn[1], [yj[1, c, f] for f in range(5)], 1))
            if c == 0:
                back[2] = add3(back[2], node.face(adj[2], vn[2], zbot, -1))
            if c == 3:
                back[2] = add3(back[2], node.face(adj[2], vn[2], ztop, 1))
            grads = node.gradient()
            for f in range(5):
                grad_ref[f, n] = wa * grads[f]
            back0 = add3(cross(back[1], col2), cross(col1, back[2]))
            back1 = add3(cross(col2, back[0]), cross(back[2], col0))
            back2 = add3(back2, add3(cross(back[0], col1), cross(col0, back[1])))
            for k in range(3):
                j0b[b, c, k] = j0b[b, c, k] + wa * back0[k]
                j1b[a, c, k] = back1[k] if b == 0 else j1b[a, c, k] + back1[k]
        for k in range(3):
            j2b[a, b, k] = back2[k]

    @pl.when(a == 3)
    def _():
        for c in range(3):
            gx = [[[None, None], [None, None]], [[None, None], [None, None]]]
            for d in range(3):
                table = [j0b, j1b, j2b][d]
                ends = [[], []]
                for i in range(4):
                    low, high = gather_back([table[i, j, c] for j in range(4)])
                    if d:
                        low, high = WEIGHTS[i] * low, WEIGHTS[i] * high
                    ends[0].append(low)
                    ends[1].append(high)
                for j in range(2):
                    pair = gather_back(ends[j])
                    for i in range(2):
                        half = 0.5 * pair[i]
                        low = [(0, i, j), (i, 0, j), (i, j, 0)][d]
                        high = [(1, i, j), (i, 1, j), (i, j, 1)][d]
                        gx[high[0]][high[1]][high[2]] = add(gx[high[0]][high[1]][high[2]], half)
                        gx[low[0]][low[1]][low[2]] = add(gx[low[0]][low[1]][low[2]], -half)
            for e1 in range(2):
                for e2 in range(2):
                    g_ref[e1, c, e2] = gx[e1][e2][0] + pltpu.roll(gx[e1][e2][1], 1, 1)


def face_kernel(flags_ref, u_ref, lam_ref, disp_ref, lower_ref, upper_ref, g_ref, grad_in_ref, grad_ref, part_ref, row_ref):
    side = pl.program_id(0)
    is_first = flags_ref[0] == 1
    is_last = flags_ref[1] == 1

    def run(received_ref, wall, scale, sigma):
        col1 = [[None] * 3 for _ in range(4)]
        col2 = [[None] * 3 for _ in range(4)]
        for k in range(3):
            x = [[corner(disp_ref, k, side, e2, e3) for e3 in range(2)] for e2 in range(2)]
            along1 = spread(0.5 * (x[1][0] - x[0][0]), 0.5 * (x[1][1] - x[0][1]))
            along2 = spread(0.5 * (x[0][1] - x[0][0]), 0.5 * (x[1][1] - x[1][0]))
            for i in range(4):
                col1[i][k] = along1[i] + 0.5 if k == 1 else along1[i]
                col2[i][k] = along2[i] + 0.5 if k == 2 else along2[i]
        back1 = [None] * 4
        back2 = [None] * 4
        for b in range(4):
            for c in range(4):
                n = 4 * b + c
                weight = float(WEIGHTS[b] * WEIGHTS[c])
                u = [u_ref[f, n] for f in range(5)]
                own = [lam_ref[f, n] for f in range(5)]
                normal = cross(col1[c], col2[b])
                if wall:
                    inverse, v, v2, p, ep = primitives(u)
                    vn = dot3(normal, v)
                    m = u[1:4]
                    jump = [-weight * own[f] for f in range(1, 4)]
                    square = dot3(normal, normal)
                    root = lax.rsqrt(square)
                    rate = vn * (root * root)
                    q = u[0] * vn
                    level = dot3(jump, normal)
                    slope = 2.0 * (rate - root)
                    phi = q * (rate - 2.0 * root) + p
                    lk = level * slope
                    along = lk * q * (root * root)
                    grads = [level * (0.2 * v2 - rate * vn)]
                    for k in range(3):
                        grads.append(lk * normal[k] - (0.4 * level) * v[k])
                    grads.append(0.4 * level)
                    back = [jump[k] * phi + lk * m[k] - along * normal[k] for k in range(3)]
                else:
                    node = Node(u)
                    vn = dot3(normal, node.v)
                    factor = scale * weight
                    jump = [factor * (own[f] - received_ref[f, n]) for f in range(5)]
                    back = node.face(normal, vn, jump, sigma)
                    grads = node.gradient()
                for f in range(5):
                    grad_ref[f, n] = grad_in_ref[f, n] + grads[f]
                back1[c] = add3(back1[c], cross(col2[b], back))
                back2[b] = add3(back2[b], cross(back, col1[c]))
        for k in range(3):
            low1, high1 = gather_back([back1[i][k] for i in range(4)])
            low2, high2 = gather_back([back2[i][k] for i in range(4)])
            gx = [[-0.5 * (low1 + low2), 0.5 * (low2 - high1)], [0.5 * (low1 - high2), 0.5 * (high1 + high2)]]
            near = g_ref[0, k, 0] + gx[0][0] + pltpu.roll(gx[0][1], 1, 1)
            far = g_ref[0, k, 1] + gx[1][0] + pltpu.roll(gx[1][1], 1, 1)
            rows = lax.broadcasted_iota(jnp.int32, (8, 128), 0)
            part_ref[0, k] = near + jnp.where(rows == 0, 0.0, pltpu.roll(far, 1, 0))
            row_ref[0, k : k + 1, :] = far[7:8, :]

    @pl.when((side == 0) & is_first)
    def _():
        run(None, True, None, None)

    @pl.when((side == 0) & jnp.logical_not(is_first))
    def _():
        run(lower_ref, False, -0.5, -1)

    @pl.when(side == 1)
    def _():
        run(upper_ref, False, jnp.where(is_last, F32(1.0), F32(0.5)), jnp.where(is_last, F32(0.0), F32(1.0)))


def volume_call(u, lam, disp, yup, ydn):
    tile = (8, 128)
    whole = lambda shape: pl.BlockSpec(shape, lambda a: (0,) * len(shape))
    return pl.pallas_call(
        volume_kernel,
        grid=(4,),
        in_specs=[
            pl.BlockSpec((5, 16) + tile, lambda a: (0, a, 0, 0)),
            whole(lam.shape),
            whole(disp.shape),
            whole(yup.shape),
            whole(ydn.shape),
        ],
        out_specs=[
            pl.BlockSpec((5, 16) + tile, lambda a: (0, a, 0, 0)),
            whole((2, 3, 2) + tile),
        ],
        out_shape=[
            jax.ShapeDtypeStruct((5, 64) + tile, F32),
            jax.ShapeDtypeStruct((2, 3, 2) + tile, F32),
        ],
        scratch_shapes=[pltpu.VMEM((4, 4, 3) + tile, F32)] * 6
        + [
            pltpu.VMEM((4, 16, 5) + tile, F32),
            pltpu.VMEM((16, 5) + tile, F32),
            pltpu.VMEM((2, 4, 5) + tile, F32),
        ],
        name="volume",
    )(u, lam, disp, yup, ydn)


def face_call(flags, u, lam, disp, lower, upper, g, grad):
    tile = (8, 128)
    whole = lambda shape: pl.BlockSpec(shape, lambda a: (0,) * len(shape))
    side_block = pl.BlockSpec((5, 16) + tile, lambda a: (0, 3 * a, 0, 0))
    return pl.pallas_call(
        face_kernel,
        grid=(2,),
        in_specs=[
            pl.BlockSpec(memory_space=pltpu.SMEM),
            side_block,
            side_block,
            whole(disp.shape),
            whole(lower.shape),
            whole(upper.shape),
            pl.BlockSpec((1, 3, 2) + tile, lambda a: (a, 0, 0, 0, 0)),
            side_block,
        ],
        out_specs=[
            side_block,
            pl.BlockSpec((1, 3) + tile, lambda a: (a, 0, 0, 0)),
            pl.BlockSpec((1, 3, 128), lambda a: (a, 0, 0)),
        ],
        out_shape=[
            jax.ShapeDtypeStruct((5, 64) + tile, F32),
            jax.ShapeDtypeStruct((2, 3) + tile, F32),
            jax.ShapeDtypeStruct((2, 3, 128), F32),
        ],
        input_output_aliases={7: 0},
        name="faces",
    )(flags, u, lam, disp, lower, upper, g, grad)


def bernstein(parameter, degree):
    orders = jnp.arange(degree + 1).astype(jnp.float32)[:, None]
    binomials = jnp.asarray(
        np.array([math.comb(degree, member) for member in range(degree + 1)]), jnp.float32
    )[:, None]
    return (
        binomials
        * jnp.power(parameter[None, :], orders)
        * jnp.power(1.0 - parameter[None, :], degree - orders)
    )


def bernstein_rows(sensitivity, coords):
    row_count = sensitivity.shape[1]
    along_u = bernstein(coords[0], LU - 1)
    along_v = bernstein(coords[1], LV - 1)
    along_w = bernstein(coords[2], LW - 1)
    inner_rows = (
        sensitivity[:, None, None, :] * along_v[None, :, None, :] * along_w[None, None, :, :]
    ).reshape(3 * LV * LW, row_count)
    return (along_u, inner_rows)


def shift_px(payload, step):
    length = lax.axis_size("px")
    pairs = [(i, i + step) for i in range(length) if 0 <= i + step < length]
    return lax.ppermute(payload, "px", pairs)


def shift_py(payload, step):
    length = lax.axis_size("py")
    return lax.ppermute(payload, "py", [(i, (i + step) % length) for i in range(length)])


def per_device(flow_state, adjoint, displacement, lattice_block, lattice_coords):
    u = flow_state.reshape(5, 64, 8, 128)
    lam = adjoint.reshape(5, 64, 8, 128)
    index = lax.axis_index("px")
    flags = jnp.stack([index == 0, index == lax.axis_size("px") - 1]).astype(jnp.int32)
    upper = shift_px(lam[:, 0:16], -1)
    lower = shift_px(lam[:, 48:64], 1)
    cube = lam.reshape(5, 4, 4, 4, 8, 128)
    yup = shift_py(cube[:, :, 0, :, 0, :].reshape(80, 128), -1)
    ydn = shift_py(cube[:, :, 3, :, 7, :].reshape(80, 128), 1)
    grad, g = volume_call(u, lam, displacement, yup, ydn)
    grad, part, rows = face_call(flags, u, lam, displacement, lower, upper, g, grad)
    rows = shift_py(rows, 1)
    part = part.at[:, :, 0, :].add(rows)
    owned = part[0] + shift_px(part[1], 1)
    owned_vertex_sensitivity = owned.reshape(3, 1, 8, 128)
    sensitivity = owned.reshape(3, -1)
    row_count = sensitivity.shape[1]
    coords = lattice_coords.reshape(3, row_count)
    block_ids = lattice_block.reshape(row_count)
    device_count = lax.axis_size("px") * lax.axis_size("py")
    capacity = max(2, 2 * row_count // device_count)
    block_range = jnp.arange(device_count, dtype=jnp.int32)
    matches = (block_ids[:, None] == block_range[None, :]).astype(jnp.int32)
    running_counts = jnp.cumsum(matches, axis=0)
    slot_ranks = jnp.sum(matches * (running_counts - 1), axis=1)
    targets = block_ids * capacity + slot_ranks
    slot_range = jnp.arange(device_count * capacity, dtype=jnp.int32)
    placement = (targets[:, None] == slot_range[None, :]).astype(jnp.float32)
    payload = jnp.concatenate([sensitivity, coords], axis=0)
    buffer = jnp.dot(payload, placement, precision=HIGHEST, preferred_element_type=jnp.float32)
    received = lax.all_to_all(buffer, ("px", "py"), split_axis=1, concat_axis=1, tiled=True)
    along_u, inner_rows = bernstein_rows(received[0:3], received[3:6])
    product = jnp.einsum("ar,jr->aj", along_u, inner_rows, precision=HIGHEST)
    block_grad = jnp.transpose(product.reshape(LU, 3, LV * LW), (1, 0, 2)).reshape(3, LU * LV * LW)
    lattice_grad = block_grad.reshape(1, 1, 3, LU * LV * LW)
    return (grad.reshape(5, 64, 1, 8, 128), owned_vertex_sensitivity, lattice_grad)


def solution(mesh):
    in_specs = (
        P(None, None, "px", "py", None),
        P(None, None, "px", "py", None),
        P(None, "px", "py", None),
        P("px", "py", None, None),
        P("px", "py", None, None),
    )
    out_specs = (
        P(None, None, "px", "py", None),
        P(None, "px", "py", None),
        P("px", "py", None, None),
    )
    return jax.shard_map(
        per_device, mesh=mesh, in_specs=in_specs, out_specs=out_specs, check_vma=False
    )
```

profile of v0, /device:TPU:0, one launch (start us, length us, event | category | flops | bytes accessed | tf_op | source)
XLA Modules:
  0.0 71.4 jit_solution(16054160969587962258)
XLA Ops:
  0.7 1.1 %fusion.29 = (f32[5,16,8,128]{3,2,1,0:T(8,128)S(1)}, f32[5,16,8,128]{3,2,1,0:T(8,128)S(1)}) fusion(f32[5,64,8,128]{3,2,1,0:T(8,128)} %bitcast.63), kind=kLoop, calls=%fused_computation.52 | loop fusion | bytes 1310720 | tf_op jit(solution)/shard_map/slice | solution.py:450
  1.8 4.9 %collective-permute-start = (f32[5,16,8,128]{3,2,1,0:T(8,128)S(1)}, f32[5,16,8,128]{3,2,1,0:T(8,128)S(1)}, u32[]{:S(2)}, u32[]{:S(2)}) collective-permute-start(f32[5,16,8,128]{3,2,1,0:T(8,128)S(1)} %get-tuple-element.43), channel_id=1, source_target_pairs={{0,4},{4,8},{8,12},{12,16},{16,20},{20,24},{24,28},{1,5},{5,9},{9,... | collective-permute-start | bytes 983048 | tf_op jit(solution)/shard_map/ppermute | solution.py:437
  6.7 1.3 %collective-permute-start.1 = (f32[5,16,8,128]{3,2,1,0:T(8,128)S(1)}, f32[5,16,8,128]{3,2,1,0:T(8,128)S(1)}, u32[]{:S(2)}, u32[]{:S(2)}) collective-permute-start(f32[5,16,8,128]{3,2,1,0:T(8,128)S(1)} %get-tuple-element.42), channel_id=1, source_target_pairs={{4,0},{8,4},{12,8},{16,12},{20,16},{24,20},{28,24},{5,1},{9,5},{13... | collective-permute-start | bytes 983048 | tf_op jit(solution)/shard_map/ppermute | solution.py:437
  8.0 1.1 %fusion.28 = (f32[5,4,1,4,1,128]{5,4,3,2,1,0:T(1,128)S(1)}, f32[5,4,1,4,1,128]{5,4,3,2,1,0:T(1,128)S(1)}) fusion(f32[5,4,4,4,8,128]{5,4,3,2,1,0:T(8,128)} %bitcast.64), kind=kLoop, calls=%fused_computation.51 | loop fusion | bytes 163840 | tf_op jit(solution)/shard_map/slice | solution.py:454
  10.5 9.0 %reduce-window.6 = s32[32,8,128]{2,1,0:T(8,128)S(1)} reduce-window(s32[32,8,128]{2,1,0:T(8,128)S(1)} %fusion.15, s32[]{:T(128)} %constant.48.clone.1), window={size=1x1x128 pad=0_0x0_0x127_0}, to_apply=%region_0.0 | reduce-window | flops 4161536 | bytes 262148 | tf_op jit(solution)/shard_map/reduce-window
  21.9 6.4 %volume.1 = (f32[5,64,8,128]{3,2,1,0:T(8,128)}, f32[2,3,2,8,128]{4,3,2,1,0:T(8,128)}) custom-call(f32[5,64,8,128]{3,2,1,0:T(8,128)} %bitcast.67, f32[5,64,8,128]{3,2,1,0:T(8,128)} %bitcast.65, f32[3,2,9,128]{3,2,1,0:T(8,128)} %copy.47.disp_ref, f32[80,128]{1,0:T(8,128)} %copy-done.3, f32[80,128]{1,0:T(8,128)} %copy-done.4), custom_call_target="tpu_custom_call" | custom-call | tf_op jit(solution)/shard_map/volume/pallas_call | solution.py:351
  29.2 3.0 %faces.1 = (f32[5,64,8,128]{3,2,1,0:T(8,128)}, f32[2,3,8,128]{3,2,1,0:T(8,128)}, f32[2,3,128]{2,1,0:T(4,128)}) custom-call(s32[2]{0:T(128)} %add_convert_fusion.flags_ref, f32[5,64,8,128]{3,2,1,0:T(8,128)} %bitcast.68, f32[5,64,8,128]{3,2,1,0:T(8,128)} %bitcast.66, f32[3,2,9,128]{3,2,1,0:T(8,128)} %copy.47.disp_ref, ...), custom_call_target="tpu_custom_call", output_to_operand_aliasing={{0}: (7, {})} | custom-call | tf_op jit(solution)/shard_map/faces/pallas_call | solution.py:383
  32.2 1.1 %collective-permute-start.4 = (f32[2,3,128]{2,1,0:T(4,128)}, f32[2,3,128]{2,1,0:T(4,128)S(1)}, u32[]{:S(2)}, u32[]{:S(2)}) collective-permute-start(f32[2,3,128]{2,1,0:T(4,128)} %get-tuple-element.24), channel_id=1, source_target_pairs={{0,1},{1,2},{2,3},{3,0},{4,5},{5,6},{6,7},{7,4},{8,9},{9,10},{10,1... | collective-permute-start | bytes 9224 | tf_op jit(solution)/shard_map/ppermute | solution.py:442
  33.3 0.7 %copy.48 = f32[2,3,8,128]{3,1,0,2:T(4,128)S(1)} copy(f32[2,3,8,128]{3,2,1,0:T(8,128)} %get-tuple-element.23) | data formatting | bytes 49152 | tf_op jit(solution)/shard_map/faces/pallas_call | solution.py:383
  34.1 1.5 %collective-permute-done.4 = f32[2,3,128]{2,1,0:T(4,128)S(1)} collective-permute-done((f32[2,3,128]{2,1,0:T(4,128)}, f32[2,3,128]{2,1,0:T(4,128)S(1)}, u32[]{:S(2)}, u32[]{:S(2)}) %collective-permute-start.4) | collective-permute-done | bytes 3104 | tf_op jit(solution)/shard_map/ppermute | solution.py:442
  35.5 1.4 %scatter-add.4 = f32[2,3,8,128]{3,2,1,0:T(8,128)} dynamic-update-slice(f32[2,3,8,128]{3,2,1,0:T(8,128)} %get-tuple-element.23, f32[2,3,1,128]{3,2,1,0:T(1,128)S(1)} %copy.49, s32[]{:T(128)} %constant.48.clone.1, s32[]{:T(128)} %constant.48.clone.1, s32[]{:T(128)} %constant.48.clone.1, s32[]{:T(128)} %constant.48.clone.1) | dynamic-update-slice | bytes 6148 | tf_op jit(solution)/shard_map/scatter-add | solution.py:458
  36.9 0.7 slice_bitcast_fusion
  37.6 4.4 %collective-permute-start.5 = (f32[3,8,128]{2,1,0:T(8,128)S(1)}, f32[3,8,128]{2,1,0:T(8,128)S(1)}, u32[]{:S(2)}, u32[]{:S(2)}) collective-permute-start(f32[3,8,128]{2,1,0:T(8,128)S(1)} %slice_bitcast_fusion), channel_id=1, source_target_pairs={{0,4},{4,8},{8,12},{12,16},{16,20},{20,24},{24,28},{1,5},{5,9},{9,... | collective-permute-start | bytes 36872 | tf_op jit(solution)/shard_map/ppermute | solution.py:437
  42.0 1.4 %collective-permute-done.5 = f32[3,8,128]{2,1,0:T(8,128)S(1)} collective-permute-done((f32[3,8,128]{2,1,0:T(8,128)S(1)}, f32[3,8,128]{2,1,0:T(8,128)S(1)}, u32[]{:S(2)}, u32[]{:S(2)}) %collective-permute-start.5) | collective-permute-done | bytes 12320 | tf_op jit(solution)/shard_map/ppermute | solution.py:437
  43.4 1.3 %fusion.25 = (f32[1,3,8,128]{3,2,1,0:T(8,128)S(1)}, f32[3,1,8,128]{3,2,1,0:T(8,128)}) fusion(f32[3,8,128]{2,1,0:T(8,128)S(1)} %collective-permute-done.5, f32[2,3,8,128]{3,2,1,0:T(8,128)} %scatter-add.4), kind=kLoop, calls=%fused_computation.38 | loop fusion | flops 3072 | bytes 49152
  44.7 2.8 %fusion = f32[6,2048]{1,0:T(8,128)S(1)} fusion(s32[1024]{0:T(1024)S(1)} %multiply_add_fusion, f32[3,1024]{1,0:T(4,128)S(1)} %bitcast.80, f32[3,1024]{1,0:T(4,128)S(1)} %bitcast.81), kind=kOutput, calls=%fused_computation.1 | convolution fusion | flops 153098240 | bytes 77824 | tf_op jit(solution)/shard_map/dot_general | solution.py:475
  47.6 0.7 %reshape.310 = f32[32,1,384]{2,1,0:T(1,128)} reshape(f32[32,6,64]{2,1,0:T(8,128)S(1)} %bitcast.70) | data formatting | bytes 98304
  48.3 7.4 %all-to-all-start = ((f32[32,1,384]{2,1,0:T(1,128)}), f32[32,1,384]{2,1,0:T(1,128)S(1)}, u32[]{:S(2)}, u32[]{:S(2)}) async-start(f32[32,1,384]{2,1,0:T(1,128)} %reshape.310), calls=%async_computation | async-start | bytes 98304 | tf_op jit(solution)/shard_map/all_to_all | solution.py:476
  55.8 7.3 %all-to-all-done = f32[32,1,384]{2,1,0:T(1,128)S(1)} async-done(((f32[32,1,384]{2,1,0:T(1,128)}), f32[32,1,384]{2,1,0:T(1,128)S(1)}, u32[]{:S(2)}, u32[]{:S(2)}) %all-to-all-start) | async-done | bytes 49184 | tf_op jit(solution)/shard_map/all_to_all | solution.py:476
  63.6 0.8 %reduce.14 = f32[32,384]{1,0:T(8,128)S(1)} reduce(f32[32,1,384]{2,1,0:T(1,128)S(1)} %all-to-all-done, f32[]{:T(128)} %broadcast.210), dimensions={1}, to_apply=%all_to_all.7.reduce_sub_computation | reduce | bytes 98308 | tf_op jit(solution)/shard_map/all_to_all | solution.py:476
  65.6 1.5 %mul.117 = f32[3,72,2048]{2,1,0:T(8,128)} reshape(f32[3,12,6,2048]{3,2,1,0:T(8,128)S(1)} %mul.116) | data formatting | bytes 3538944 | tf_op jit(solution)/shard_map/mul | solution.py:429
  67.6 0.9 %copy-done = f32[3,72,2048]{2,1,0:T(8,128)S(1)} copy-done((f32[3,72,2048]{2,1,0:T(8,128)S(1)}, f32[3,72,2048]{2,1,0:T(8,128)}, u32[]{:S(2)}) %copy-start) | copy-done | bytes 1769496
  68.6 2.1 %fusion.4 = f32[3,12,72]{2,1,0:T(8,128)S(1)} fusion(f32[3,72,2048]{2,1,0:T(8,128)S(1)} %copy-done, f32[72,2048]{1,0:T(8,128)S(1)} %mul.122, f32[12]{0:T(128)S(1)} %broadcast_subtract_fusion.4, f32[2048]{0:T(1024)S(1)} %broadcast_subtract_fusion.2, f32[12]{0:T(128)S(1)} %iota_convert_fusion.1, f32[2048]{0:T(1024)S(1)} %pow.100, f32[12]{0:T(128)S(1)} %copy-done.8), kind=kOutput, calls=%fused_computation.5 | convolution fusion | flops 64192512 | bytes 2386192 | tf_op jit(solution)/shard_map/ar,jr->aj/dot_general | solution.py:478
  70.6 0.7 %reshape_reshape.8 = f32[1,1,3,864]{3,1,2,0:T(1,128)} reshape(f32[3,12,72]{2,1,0:T(8,128)S(1)} %fusion.4) | data formatting | bytes 20736 | tf_op jit(solution)/shard_map/reshape;reshape | solution.py:480
  (64 shorter events, 6.9 us)
Async XLA Ops:
  0.6 19.4 %copy-start.5 = (s32[1,1,1024,1]{2,3,1,0:T(1,128)S(1)}, s32[1,1,1024,1]{2,3,1,0:T(1,128)}, u32[]{:S(2)}) copy-start(s32[1,1,1024,1]{2,3,1,0:T(1,128)} %param.13) | copy-start | bytes 12292
  0.6 20.1 %copy-start.6 = (f32[3,2,9,128]{3,1,2,0:T(2,128)S(1)}, f32[3,2,9,128]{3,1,2,0:T(2,128)}, u32[]{:S(2)}) copy-start(f32[3,2,9,128]{3,1,2,0:T(2,128)} %param.12) | copy-start | bytes 82948
  1.8 26.6 %collective-permute-start = (f32[5,16,8,128]{3,2,1,0:T(8,128)S(1)}, f32[5,16,8,128]{3,2,1,0:T(8,128)S(1)}, u32[]{:S(2)}, u32[]{:S(2)}) collective-permute-start(f32[5,16,8,128]{3,2,1,0:T(8,128)S(1)} %get-tuple-element.43), channel_id=1, source_target_pairs={{0,4},{4,8},{8,12},{12,16},{16,20},{20,24},{24,28},{1,5},{5,9},{9,... | collective-permute-start | bytes 983048 | tf_op jit(solution)/shard_map/ppermute | solution.py:437
  6.7 21.7 %collective-permute-start.1 = (f32[5,16,8,128]{3,2,1,0:T(8,128)S(1)}, f32[5,16,8,128]{3,2,1,0:T(8,128)S(1)}, u32[]{:S(2)}, u32[]{:S(2)}) collective-permute-start(f32[5,16,8,128]{3,2,1,0:T(8,128)S(1)} %get-tuple-element.42), channel_id=1, source_target_pairs={{4,0},{8,4},{12,8},{16,12},{20,16},{24,20},{28,24},{5,1},{9,5},{13... | collective-permute-start | bytes 983048 | tf_op jit(solution)/shard_map/ppermute | solution.py:437
  9.1 12.2 %collective-permute-start.2 = (f32[80,128]{1,0:T(8,128)S(1)}, f32[80,128]{1,0:T(8,128)S(1)}, u32[]{:S(2)}, u32[]{:S(2)}) collective-permute-start(f32[80,128]{1,0:T(8,128)S(1)} %bitcast.75), channel_id=1, source_target_pairs={{0,3},{1,0},{2,1},{3,2},{4,7},{5,4},{6,5},{7,6},{8,11},{9,8},{10,9... | collective-permute-start | bytes 122888 | tf_op jit(solution)/shard_map/ppermute | solution.py:442
  9.8 11.5 %collective-permute-start.3 = (f32[80,128]{1,0:T(8,128)S(1)}, f32[80,128]{1,0:T(8,128)S(1)}, u32[]{:S(2)}, u32[]{:S(2)}) collective-permute-start(f32[80,128]{1,0:T(8,128)S(1)} %bitcast.74), channel_id=1, source_target_pairs={{0,1},{1,2},{2,3},{3,0},{4,5},{5,6},{6,7},{7,4},{8,9},{9,10},{10,1... | collective-permute-start | bytes 122888 | tf_op jit(solution)/shard_map/ppermute | solution.py:442
  21.3 0.6 copy-start.3
  21.3 0.6 copy-start.4
  28.4 0.7 %copy-start.1 = (f32[5,16,8,128]{3,2,1,0:T(8,128)}, f32[5,16,8,128]{3,2,1,0:T(8,128)S(1)}, u32[]{:S(2)}) copy-start(f32[5,16,8,128]{3,2,1,0:T(8,128)S(1)} %collective-permute-done.lower_ref) | copy-start | bytes 983044
  28.4 0.8 %copy-start.2 = (f32[5,16,8,128]{3,2,1,0:T(8,128)}, f32[5,16,8,128]{3,2,1,0:T(8,128)S(1)}, u32[]{:S(2)}) copy-start(f32[5,16,8,128]{3,2,1,0:T(8,128)S(1)} %collective-permute-done.1.upper_ref) | copy-start | bytes 983044
  29.2 12.8 %copy-start.7 = (f32[1,1,3,1024]{3,1,2,0:T(1,128)S(1)}, f32[1,1,3,1024]{3,1,2,0:T(1,128)}, u32[]{:S(2)}) copy-start(f32[1,1,3,1024]{3,1,2,0:T(1,128)} %param.14) | copy-start | bytes 36868
  32.2 3.3 %collective-permute-start.4 = (f32[2,3,128]{2,1,0:T(4,128)}, f32[2,3,128]{2,1,0:T(4,128)S(1)}, u32[]{:S(2)}, u32[]{:S(2)}) collective-permute-start(f32[2,3,128]{2,1,0:T(4,128)} %get-tuple-element.24), channel_id=1, source_target_pairs={{0,1},{1,2},{2,3},{3,0},{4,5},{5,6},{6,7},{7,4},{8,9},{9,10},{10,1... | collective-permute-start | bytes 9224 | tf_op jit(solution)/shard_map/ppermute | solution.py:442
  37.6 5.8 %collective-permute-start.5 = (f32[3,8,128]{2,1,0:T(8,128)S(1)}, f32[3,8,128]{2,1,0:T(8,128)S(1)}, u32[]{:S(2)}, u32[]{:S(2)}) collective-permute-start(f32[3,8,128]{2,1,0:T(8,128)S(1)} %slice_bitcast_fusion), channel_id=1, source_target_pairs={{0,4},{4,8},{8,12},{12,16},{16,20},{20,24},{24,28},{1,5},{5,9},{9,... | collective-permute-start | bytes 36872 | tf_op jit(solution)/shard_map/ppermute | solution.py:437
  44.7 20.2 %copy-start.8 = (f32[12]{0:T(128)S(1)}, f32[12]{0:T(128)}, u32[]{:S(2)}) copy-start(f32[12]{0:T(128)} %constant.55.clone) | copy-start | bytes 148
  48.3 14.8 %all-to-all-start = ((f32[32,1,384]{2,1,0:T(1,128)}), f32[32,1,384]{2,1,0:T(1,128)S(1)}, u32[]{:S(2)}, u32[]{:S(2)}) async-start(f32[32,1,384]{2,1,0:T(1,128)} %reshape.310), calls=%async_computation | async-start | bytes 98304 | tf_op jit(solution)/shard_map/all_to_all | solution.py:476
  65.6 1.6 %copy-start.9 = (f32[6]{0:T(128)S(1)}, f32[6]{0:T(128)}, u32[]{:S(2)}) copy-start(f32[6]{0:T(128)} %constant.56.clone) | copy-start | bytes 76
  67.1 1.5 %copy-start = (f32[3,72,2048]{2,1,0:T(8,128)S(1)}, f32[3,72,2048]{2,1,0:T(8,128)}, u32[]{:S(2)}) copy-start(f32[3,72,2048]{2,1,0:T(8,128)} %mul.117) | copy-start | bytes 5308420
where the time goes:
time: 72 us; the launch traced here: 71.4 us
  starting transfers between devices  19.8 us (28%)
  other arithmetic  13.3 us (18%)
  local copies, waits for them, and re-layouts  12.9 us (18%)
  waiting for transfers between devices  10.2 us (14%)
  Pallas kernels  9.44 us (13%)
  matrix products  4.83 us (7%)
  between operations  0.92 us (1%)
    ppermute x3, starting transfers between devices, shift_px(): return lax.ppermute(payload, 'px', pairs)  10.6 us
    another operation x2, other arithmetic  9.04 us
    all_to_all x1, starting transfers between devices, per_device(): lax.all_to_all(buffer, ('px', 'py'), split_axis=1, concat_axis=1, tiled=T...  7.45 us
    all_to_all x1, waiting for transfers between devices, per_device(): lax.all_to_all(buffer, ('px', 'py'), split_axis=1, concat_axis=1, tiled=T...  7.32 us
    pallas_call x1, Pallas kernels, volume_call(): pl.pallas_call(volume_kernel, grid=(4,), in_specs=[pl.BlockSpec((5, 16) +...  6.44 us
    unnamed x25, local copies, waits for them, and re-layouts  3.81 us
    pallas_call x1, Pallas kernels, face_call(): pl.pallas_call(face_kernel, grid=(2,), in_specs=[pl.BlockSpec(memory_spac...  2.99 us
    dot_general x1, matrix products, per_device(): jnp.dot(payload, placement, precision=HIGHEST, preferred_element_type=jnp...  2.76 us
  transfers between devices with their start and end apart: 7, of which 3 were waited for; matrix products, arithmetic and copies ran while one was open for 19% of the time, Pallas kernels for 9%

commit v1 on v0

--- a/solution.py
+++ b/solution.py
@@ -12,7 +12,6 @@
 LU = 12
 LV = 12
 LW = 6
-HIGHEST = lax.Precision.HIGHEST
 F32 = jnp.float32
 POINTS = [-1.0, -1.0 / math.sqrt(5.0), 1.0 / math.sqrt(5.0), 1.0]
 WEIGHTS = [1.0 / 6.0, 5.0 / 6.0, 5.0 / 6.0, 1.0 / 6.0]
@@ -268,12 +267,28 @@
                     g_ref[e1, c, e2] = gx[e1][e2][0] + pltpu.roll(gx[e1][e2][1], 1, 1)
 
 
-def face_kernel(flags_ref, u_ref, lam_ref, disp_ref, lower_ref, upper_ref, g_ref, grad_in_ref, grad_ref, part_ref, row_ref):
-    side = pl.program_id(0)
-    is_first = flags_ref[0] == 1
-    is_last = flags_ref[1] == 1
-
-    def run(received_ref, wall, scale, sigma):
+def face_kernel(nb, cap, px, u_ref, lam_ref, disp_ref, lower_ref, upper_ref, g_ref, blk_ref, yup_ref, far_ref, rank_ref, cpack_ref, grad_in_ref, grad_ref, buf_ref, part_ref, row_ref, ubuf, lbuf, rbuf, gbuf, lhs, rhs, sem):
+    index = lax.axis_index("px")
+    is_first = index == 0
+    is_last = index == px - 1
+    copies = []
+    for side in range(2):
+        nodes = pl.ds(48 * side, 16)
+        sources = [
+            (u_ref.at[:, nodes], ubuf),
+            (lam_ref.at[:, nodes], lbuf),
+            (upper_ref if side else lower_ref, rbuf),
+            (grad_in_ref.at[:, nodes], gbuf),
+        ]
+        group = [
+            pltpu.make_async_copy(source, target.at[side], sem.at[side, i])
+            for i, (source, target) in enumerate(sources)
+        ]
+        for copy in group:
+            copy.start()
+        copies.append(group)
+
+    def run(side, wall, scale, sigma):
         col1 = [[None] * 3 for _ in range(4)]
         col2 = [[None] * 3 for _ in range(4)]
         for k in range(3):
@@ -289,8 +304,8 @@
             for c in range(4):
                 n = 4 * b + c
                 weight = float(WEIGHTS[b] * WEIGHTS[c])
-                u = [u_ref[f, n] for f in range(5)]
-                own = [lam_ref[f, n] for f in range(5)]
+                u = [ubuf[side, f, n] for f in range(5)]
+                own = [lbuf[side, f, n] for f in range(5)]
                 normal = cross(col1[c], col2[b])
                 if wall:
                     inverse, v, v2, p, ep = primitives(u)
@@ -315,34 +330,205 @@
                     node = Node(u)
                     vn = dot3(normal, node.v)
                     factor = scale * weight
-                    jump = [factor * (own[f] - received_ref[f, n]) for f in range(5)]
+                    jump = [factor * (own[f] - rbuf[side, f, n]) for f in range(5)]
                     back = node.face(normal, vn, jump, sigma)
                     grads = node.gradient()
                 for f in range(5):
-                    grad_ref[f, n] = grad_in_ref[f, n] + grads[f]
+                    gbuf[side, f, n] = gbuf[side, f, n] + grads[f]
                 back1[c] = add3(back1[c], cross(col2[b], back))
                 back2[b] = add3(back2[b], cross(back, col1[c]))
+        rows = lax.broadcasted_iota(jnp.int32, (8, 128), 0)
         for k in range(3):
             low1, high1 = gather_back([back1[i][k] for i in range(4)])
             low2, high2 = gather_back([back2[i][k] for i in range(4)])
             gx = [[-0.5 * (low1 + low2), 0.5 * (low2 - high1)], [0.5 * (low1 - high2), 0.5 * (high1 + high2)]]
-            near = g_ref[0, k, 0] + gx[0][0] + pltpu.roll(gx[0][1], 1, 1)
-            far = g_ref[0, k, 1] + gx[1][0] + pltpu.roll(gx[1][1], 1, 1)
-            rows = lax.broadcasted_iota(jnp.int32, (8, 128), 0)
-            part_ref[0, k] = near + jnp.where(rows == 0, 0.0, pltpu.roll(far, 1, 0))
-            row_ref[0, k : k + 1, :] = far[7:8, :]
-
-    @pl.when((side == 0) & is_first)
+            near = g_ref[side, k, 0] + gx[0][0] + pltpu.roll(gx[0][1], 1, 1)
+            far = g_ref[side, k, 1] + gx[1][0] + pltpu.roll(gx[1][1], 1, 1)
+            part_ref[side, k] = near + jnp.where(rows == 0, 0.0, pltpu.roll(far, 1, 0))
+            row_ref[3 * side + k : 3 * side + k + 1, :] = far[7:8, :]
+
+    for copy in copies[0]:
+        copy.wait()
+
+    @pl.when(is_first)
     def _():
-        run(None, True, None, None)
-
-    @pl.when((side == 0) & jnp.logical_not(is_first))
+        run(0, True, None, None)
+
+    @pl.when(jnp.logical_not(is_first))
     def _():
-        run(lower_ref, False, -0.5, -1)
-
-    @pl.when(side == 1)
-    def _():
-        run(upper_ref, False, jnp.where(is_last, F32(1.0), F32(0.5)), jnp.where(is_last, F32(0.0), F32(1.0)))
+        run(0, False, -0.5, -1)
+
+    back0 = pltpu.make_async_copy(gbuf.at[0], grad_ref.at[:, pl.ds(0, 16)], sem.at[0, 4])
+    back0.start()
+    for copy in copies[1]:
+        copy.wait()
+    run(1, False, jnp.where(is_last, F32(1.0), F32(0.5)), jnp.where(is_last, F32(0.0), F32(1.0)))
+    back1 = pltpu.make_async_copy(gbuf.at[1], grad_ref.at[:, pl.ds(48, 16)], sem.at[1, 4])
+    back1.start()
+
+    block_of = lax.broadcasted_iota(jnp.int32, (nb, 128), 0).astype(F32)
+    slot_of = (lax.broadcasted_iota(jnp.int32, (128, 128), 0) & (cap - 1)).astype(F32)
+    sums = []
+    for stream, count in enumerate((8, 8, 1, 1)):
+        for y in range(count):
+            block, values, ranks = [
+                (blk_ref[y : y + 1, :], lambda k: part_ref[0, k, y : y + 1, :], y),
+                (far_ref[y : y + 1, :], lambda k: part_ref[1, k, y : y + 1, :], 8 + y),
+                (yup_ref[80:81, :], lambda k: row_ref[k : k + 1, :], 16),
+                (far_ref[8:9, :], lambda k: row_ref[3 + k : 4 + k, :], 17),
+            ][stream]
+            lanes = pl.ds(128 * y, 128)
+            here = jnp.broadcast_to(block, (nb, 128)) == block_of
+            rhs[:, lanes] = jnp.where(
+                jnp.broadcast_to(rank_ref[ranks : ranks + 1, :], (128, 128)) == slot_of, 1.0, 0.0
+            ).astype(jnp.bfloat16)
+            for k in range(3):
+                row = values(k)
+                high = row.astype(jnp.bfloat16).astype(F32)
+                for part, piece in enumerate((high, row - high)):
+                    lhs[pl.ds((3 * part + k) * nb, nb), lanes] = jnp.where(
+                        here, jnp.broadcast_to(piece, (nb, 128)), 0.0
+                    ).astype(jnp.bfloat16)
+        total = lax.dot_general(
+            lhs[:, pl.ds(0, 128 * count)],
+            rhs[:, pl.ds(0, 128 * count)],
+            (((1,), (1,)), ((), ())),
+            preferred_element_type=F32,
+        )
+        total = total[0 : 3 * nb] + total[3 * nb : 6 * nb]
+        sums.append([total[k * nb : (k + 1) * nb] for k in range(3)])
+    items = [sums[stream][k] for k in range(3) for stream in range(4)]
+    items += [cpack_ref[pl.ds(k * nb, nb), :] for k in range(3)]
+    per_row = 128 // cap
+    height = buf_ref.shape[0] // nb
+    position = lax.broadcasted_iota(jnp.int32, (nb, 128), 1) // cap
+    for r in range(height):
+        inside = items[r * per_row : (r + 1) * per_row]
+        value = inside[0]
+        for i, item in enumerate(inside[1:], 1):
+            value = jnp.where(position == i, item, value)
+        buf_ref[pl.ds(r, nb, stride=height), :] = value
+    back0.wait()
+    back1.wait()
+
+
+def slot_kernel(nb, cap, blk_ref, yup_ref, far_ref, coords_ref, rank_ref, cpack_ref, lhs, rhs):
+    block_of = lax.broadcasted_iota(jnp.int32, (nb, 128), 0).astype(F32)
+    k_of = lax.broadcasted_iota(jnp.int32, (128, 256), 0)
+    z_of = lax.broadcasted_iota(jnp.int32, (128, 256), 1)
+    before = jnp.where((k_of < z_of) | (z_of >= 128), 1.0, 0.0).astype(jnp.bfloat16)
+    slot_of = (lax.broadcasted_iota(jnp.int32, (128, 128), 0) & (cap - 1)).astype(F32)
+    for stream, count in enumerate((8, 8, 1, 1)):
+        offset = jnp.zeros((nb, 128), F32)
+        for y in range(count):
+            block, slot = [
+                (blk_ref[y : y + 1, :], y),
+                (far_ref[y : y + 1, :], 8 + y),
+                (yup_ref[80:81, :], 16),
+                (far_ref[8:9, :], 17),
+            ][stream]
+            here = jnp.where(jnp.broadcast_to(block, (nb, 128)) == block_of, 1.0, 0.0)
+            counts = jnp.dot(here.astype(jnp.bfloat16), before, preferred_element_type=F32)
+            rank = jnp.sum(here * (counts[:, 0:128] + offset), axis=0, keepdims=True)
+            offset = offset + counts[:, 128:256]
+            rank_ref[slot : slot + 1, :] = rank
+            if stream == 0:
+                lanes = pl.ds(128 * y, 128)
+                rhs[:, lanes] = jnp.where(
+                    jnp.broadcast_to(rank, (128, 128)) == slot_of, 1.0, 0.0
+                ).astype(jnp.bfloat16)
+                for k in range(3):
+                    rest = coords_ref[k : k + 1, lanes]
+                    for part in range(3):
+                        piece = rest.astype(jnp.bfloat16).astype(F32)
+                        rest = rest - piece
+                        lhs[pl.ds((3 * part + k) * nb, nb), lanes] = (
+                            here * jnp.broadcast_to(piece, (nb, 128))
+                        ).astype(jnp.bfloat16)
+        if stream == 0:
+            total = lax.dot_general(
+                lhs[...], rhs[...], (((1,), (1,)), ((), ())), preferred_element_type=F32
+            )
+            cpack_ref[...] = total[0 : 3 * nb] + total[3 * nb : 6 * nb] + total[6 * nb : 9 * nb]
+
+
+def powers(t, degree):
+    out = [None, t]
+    for n in range(2, degree + 1):
+        out.append(out[n // 2] * out[n - n // 2])
+    return out
+
+
+def bernstein(t, degree):
+    up = powers(t, degree)
+    down = powers(1.0 - t, degree)
+    out = []
+    for a in range(degree + 1):
+        if a == 0:
+            out.append(down[degree])
+        elif a == degree:
+            out.append(up[degree])
+        else:
+            out.append(float(math.comb(degree, a)) * up[a] * down[degree - a])
+    return out
+
+
+def lattice_kernel(nb, cap, py, buf_ref, part_ref, yrow_ref, xrow_ref, owned_ref, out_ref, lhs, rhs):
+    rows = lax.broadcasted_iota(jnp.int32, (8, 128), 0)
+    for k in range(3):
+        beside = jnp.broadcast_to(yrow_ref[k : k + 1, :], (8, 128))
+        owned_ref[k] = part_ref[0, k] + jnp.where(rows == 0, beside, 0.0) + xrow_ref[k]
+
+    per_row = 128 // cap
+    height = buf_ref.shape[0] // nb
+    source = lax.broadcasted_iota(jnp.int32, (nb, 128), 0)
+    lane = lax.broadcasted_iota(jnp.int32, (16, 128), 1)
+
+    def item(j):
+        value = buf_ref[pl.ds(j // per_row, nb, stride=height), :]
+        at = j % per_row
+        return pltpu.roll(value, 128 - at * cap, 1) if at else value
+
+    def from_px(value):
+        return jnp.where(source >= py, pltpu.roll(value, py, 0), 0.0)
+
+    def from_py(value):
+        return jnp.where(source % py > 0, pltpu.roll(value, 1, 0), pltpu.roll(value, nb - (py - 1), 0))
+
+    def dense(value):
+        out = value[0:16]
+        for i in range(1, per_row):
+            piece = pltpu.roll(value[16 * i : 16 * (i + 1)], i * cap, 1)
+            out = jnp.where(lane // cap == i, piece, out)
+        return out
+
+    sens = []
+    for k in range(3):
+        own, above, beside, across = [item(4 * k + stream) for stream in range(4)]
+        sens.append(dense(own + from_py(beside) + from_px(above + from_py(across))))
+    u, v, w = [dense(item(12 + k)) for k in range(3)]
+    bu = bernstein(u, LU - 1)
+    bv = bernstein(v, LV - 1)
+    bw = bernstein(w, LW - 1)
+    for a in range(LU):
+        for k in range(3):
+            lhs[pl.ds(16 * (3 * a + k), 16), :] = sens[k] * bu[a]
+    for b in range(LV):
+        for c in range(LW):
+            rhs[pl.ds(16 * (LW * b + c), 16), :] = bv[b] * bw[c]
+    left = jnp.concatenate([lhs[pl.ds(i, 3 * LU, stride=16), :] for i in range(16)], axis=1)
+    right = jnp.concatenate([rhs[pl.ds(i, LV * LW, stride=16), :] for i in range(16)], axis=1)
+    left_high = left.astype(jnp.bfloat16)
+    left_low = (left - left_high.astype(F32)).astype(jnp.bfloat16)
+    right_high = right.astype(jnp.bfloat16)
+    right_low = (right - right_high.astype(F32)).astype(jnp.bfloat16)
+
+    def product(x, y):
+        return lax.dot_general(x, y, (((1,), (1,)), ((), ())), preferred_element_type=F32)
+
+    total = product(left_high, right_high) + (product(left_high, right_low) + product(left_low, right_high))
+    for a in range(LU):
+        out_ref[:, pl.ds(LV * LW * a, LV * LW)] = total[3 * a : 3 * a + 3, :]
 
 
 def volume_call(u, lam, disp, yup, ydn):
@@ -376,59 +562,60 @@
     )(u, lam, disp, yup, ydn)
 
 
-def face_call(flags, u, lam, disp, lower, upper, g, grad):
+def face_call(u, lam, disp, lower, upper, g, blk, yup, far, ranks, cpack, grad, nb, cap, px):
     tile = (8, 128)
-    whole = lambda shape: pl.BlockSpec(shape, lambda a: (0,) * len(shape))
-    side_block = pl.BlockSpec((5, 16) + tile, lambda a: (0, 3 * a, 0, 0))
+    vmem = pl.BlockSpec(memory_space=pltpu.VMEM)
+    hbm = pl.BlockSpec(memory_space=pl.ANY)
+    height = -(-15 * cap // 128)
     return pl.pallas_call(
-        face_kernel,
-        grid=(2,),
-        in_specs=[
-            pl.BlockSpec(memory_space=pltpu.SMEM),
-            side_block,
-            side_block,
-            whole(disp.shape),
-            whole(lower.shape),
-            whole(upper.shape),
-            pl.BlockSpec((1, 3, 2) + tile, lambda a: (a, 0, 0, 0, 0)),
-            side_block,
-        ],
-        out_specs=[
-            side_block,
-            pl.BlockSpec((1, 3) + tile, lambda a: (a, 0, 0, 0)),
-            pl.BlockSpec((1, 3, 128), lambda a: (a, 0, 0)),
-        ],
+        functools.partial(face_kernel, nb, cap, px),
+        in_specs=[hbm, hbm, vmem, hbm, hbm, vmem, vmem, vmem, vmem, vmem, vmem, hbm],
+        out_specs=[hbm, vmem, vmem, vmem],
         out_shape=[
             jax.ShapeDtypeStruct((5, 64) + tile, F32),
+            jax.ShapeDtypeStruct((nb * height, 128), F32),
             jax.ShapeDtypeStruct((2, 3) + tile, F32),
-            jax.ShapeDtypeStruct((2, 3, 128), F32),
-        ],
-        input_output_aliases={7: 0},
+            jax.ShapeDtypeStruct((6, 128), F32),
+        ],
+        scratch_shapes=[pltpu.VMEM((2, 5, 16) + tile, F32)] * 4
+        + [
+            pltpu.VMEM((6 * nb, 1024), jnp.bfloat16),
+            pltpu.VMEM((128, 1024), jnp.bfloat16),
+            pltpu.SemaphoreType.DMA((2, 5)),
+        ],
+        input_output_aliases={11: 0},
         name="faces",
-    )(flags, u, lam, disp, lower, upper, g, grad)
-
-
-def bernstein(parameter, degree):
-    orders = jnp.arange(degree + 1).astype(jnp.float32)[:, None]
-    binomials = jnp.asarray(
-        np.array([math.comb(degree, member) for member in range(degree + 1)]), jnp.float32
-    )[:, None]
-    return (
-        binomials
-        * jnp.power(parameter[None, :], orders)
-        * jnp.power(1.0 - parameter[None, :], degree - orders)
-    )
-
-
-def bernstein_rows(sensitivity, coords):
-    row_count = sensitivity.shape[1]
-    along_u = bernstein(coords[0], LU - 1)
-    along_v = bernstein(coords[1], LV - 1)
-    along_w = bernstein(coords[2], LW - 1)
-    inner_rows = (
-        sensitivity[:, None, None, :] * along_v[None, :, None, :] * along_w[None, None, :, :]
-    ).reshape(3 * LV * LW, row_count)
-    return (along_u, inner_rows)
+    )(u, lam, disp, lower, upper, g, blk, yup, far, ranks, cpack, grad)
+
+
+def slot_call(blk, yup, far, coords, nb, cap):
+    return pl.pallas_call(
+        functools.partial(slot_kernel, nb, cap),
+        out_shape=[
+            jax.ShapeDtypeStruct((24, 128), F32),
+            jax.ShapeDtypeStruct((3 * nb, 128), F32),
+        ],
+        scratch_shapes=[
+            pltpu.VMEM((9 * nb, 1024), jnp.bfloat16),
+            pltpu.VMEM((128, 1024), jnp.bfloat16),
+        ],
+        name="slots",
+    )(blk, yup, far, coords)
+
+
+def lattice_call(buf, part, yrow, xrow, nb, cap, py):
+    return pl.pallas_call(
+        functools.partial(lattice_kernel, nb, cap, py),
+        out_shape=[
+            jax.ShapeDtypeStruct((3, 8, 128), F32),
+            jax.ShapeDtypeStruct((3, LU * LV * LW), F32),
+        ],
+        scratch_shapes=[
+            pltpu.VMEM((16 * 3 * LU, 128), F32),
+            pltpu.VMEM((16 * LV * LW, 128), F32),
+        ],
+        name="lattice",
+    )(buf, part, yrow, xrow)
 
 
 def shift_px(payload, step):
@@ -443,42 +630,34 @@
 
 
 def per_device(flow_state, adjoint, displacement, lattice_block, lattice_coords):
+    px = lax.axis_size("px")
+    py = lax.axis_size("py")
+    nb = px * py
+    cap = 2 * 1024 // nb
     u = flow_state.reshape(5, 64, 8, 128)
     lam = adjoint.reshape(5, 64, 8, 128)
-    index = lax.axis_index("px")
-    flags = jnp.stack([index == 0, index == lax.axis_size("px") - 1]).astype(jnp.int32)
+    blk = lattice_block.reshape(8, 128).astype(F32)
+    coords = lattice_coords.reshape(3, 1024)
     upper = shift_px(lam[:, 0:16], -1)
     lower = shift_px(lam[:, 48:64], 1)
     cube = lam.reshape(5, 4, 4, 4, 8, 128)
-    yup = shift_py(cube[:, :, 0, :, 0, :].reshape(80, 128), -1)
+    yup = shift_py(jnp.concatenate([cube[:, :, 0, :, 0, :].reshape(80, 128), blk[0:1]]), -1)
     ydn = shift_py(cube[:, :, 3, :, 7, :].reshape(80, 128), 1)
+    far = shift_px(jnp.concatenate([blk, yup[80:81]]), -1)
     grad, g = volume_call(u, lam, displacement, yup, ydn)
-    grad, part, rows = face_call(flags, u, lam, displacement, lower, upper, g, grad)
-    rows = shift_py(rows, 1)
-    part = part.at[:, :, 0, :].add(rows)
-    owned = part[0] + shift_px(part[1], 1)
-    owned_vertex_sensitivity = owned.reshape(3, 1, 8, 128)
-    sensitivity = owned.reshape(3, -1)
-    row_count = sensitivity.shape[1]
-    coords = lattice_coords.reshape(3, row_count)
-    block_ids = lattice_block.reshape(row_count)
-    device_count = lax.axis_size("px") * lax.axis_size("py")
-    capacity = max(2, 2 * row_count // device_count)
-    block_range = jnp.arange(device_count, dtype=jnp.int32)
-    matches = (block_ids[:, None] == block_range[None, :]).astype(jnp.int32)
-    running_counts = jnp.cumsum(matches, axis=0)
-    slot_ranks = jnp.sum(matches * (running_counts - 1), axis=1)
-    targets = block_ids * capacity + slot_ranks
-    slot_range = jnp.arange(device_count * capacity, dtype=jnp.int32)
-    placement = (targets[:, None] == slot_range[None, :]).astype(jnp.float32)
-    payload = jnp.concatenate([sensitivity, coords], axis=0)
-    buffer = jnp.dot(payload, placement, precision=HIGHEST, preferred_element_type=jnp.float32)
-    received = lax.all_to_all(buffer, ("px", "py"), split_axis=1, concat_axis=1, tiled=True)
-    along_u, inner_rows = bernstein_rows(received[0:3], received[3:6])
-    product = jnp.einsum("ar,jr->aj", along_u, inner_rows, precision=HIGHEST)
-    block_grad = jnp.transpose(product.reshape(LU, 3, LV * LW), (1, 0, 2)).reshape(3, LU * LV * LW)
-    lattice_grad = block_grad.reshape(1, 1, 3, LU * LV * LW)
-    return (grad.reshape(5, 64, 1, 8, 128), owned_vertex_sensitivity, lattice_grad)
+    ranks, cpack = slot_call(blk, yup, far, coords, nb, cap)
+    grad, buf, part, rows = face_call(
+        u, lam, displacement, lower, upper, g, blk, yup, far, ranks, cpack, grad, nb, cap, px
+    )
+    received = lax.all_to_all(buf, ("px", "py"), split_axis=0, concat_axis=0, tiled=True)
+    yrow = shift_py(rows, 1)
+    xrow = shift_px(part[1].at[:, 0, :].add(yrow[3:6]), 1)
+    owned, lattice = lattice_call(received, part, yrow, xrow, nb, cap, py)
+    return (
+        grad.reshape(5, 64, 1, 8, 128),
+        owned.reshape(3, 1, 8, 128),
+        lattice.reshape(1, 1, 3, LU * LV * LW),
+    )
 
 
 def solution(mesh):

time: 72 us -> 51.9 us (0.72)
  other arithmetic: 13.3 us -> 0.02 us
  Pallas kernels: 9.44 us -> 15.4 us
  waiting for transfers between devices: 10.2 us -> 4.64 us
  matrix products: 4.83 us -> 0 us
  local copies, waits for them, and re-layouts: 12.9 us -> 9.03 us
  starting transfers between devices: 19.8 us -> 21.1 us
    another operation x2 -> x0, other arithmetic: 9.04 us -> none
    all_to_all x1, waiting for transfers between devices: 7.32 us -> 0.01 us  [per_device(): lax.all_to_all(buf, ('px', 'py'), split_axis=0, concat_axis=0, tiled=True)]
    pallas_call x1 -> x3, Pallas kernels: 2.99 us -> 8.9 us  [the longest x1 4.47 us: face_call(): pl.pallas_call(functools.partial(face_kernel, nb, cap, px), in_specs=[hbm...]
    dot_general x2 -> x0, matrix products: 4.83 us -> none  [the longest x1 2.76 us: per_device(): jnp.dot(payload, placement, precision=HIGHEST, preferred_element_type=jnp...]
    mul x5 -> x0, local copies, waits for them, and re-layouts: 1.99 us -> none  [bernstein_rows(): sensitivity[:, None, None, :] * along_v[None, :, None, :]]
    ppermute x3, waiting for transfers between devices: 1.48 us -> 3.25 us  [shift_py(): lax.ppermute(payload, 'py', [(i, (i + step) % length) for i in range(leng...]
    unnamed x25 -> x27, local copies, waits for them, and re-layouts: 3.81 us -> 5.24 us
    unnamed x1 -> x0, other arithmetic: 1.31 us -> none
  transfers between devices with their start and end apart: 7 -> 8, of which waited for: 3 -> 3; matrix products, arithmetic and copies ran while one was open for 19% -> 8% of each run, Pallas kernels for 9% -> 17%
where the time goes in v1:
time: 51.9 us; the launch traced here: 51 us
  starting transfers between devices  21.1 us (41%)
  Pallas kernels  15.4 us (30%)
  local copies, waits for them, and re-layouts  9.03 us (17%)
  waiting for transfers between devices  4.64 us (9%)
  between operations  0.83 us (2%)
    ppermute x4, starting transfers between devices, shift_px(): return lax.ppermute(payload, 'px', pairs)  11.8 us
    all_to_all x1, starting transfers between devices, per_device(): lax.all_to_all(buf, ('px', 'py'), split_axis=0, concat_axis=0, tiled=True)  8.09 us
    pallas_call x1, Pallas kernels, volume_call(): pl.pallas_call(volume_kernel, grid=(4,), in_specs=[pl.BlockSpec((5, 16) +...  6.45 us
    unnamed x27, local copies, waits for them, and re-layouts  5.24 us
    pallas_call x1, Pallas kernels, face_call(): pl.pallas_call(functools.partial(face_kernel, nb, cap, px), in_specs=[hbm...  4.47 us
    ppermute x3, waiting for transfers between devices, shift_py(): lax.ppermute(payload, 'py', [(i, (i + step) % length) for i in range(leng...  3.25 us
    pallas_call x1, Pallas kernels, lattice_call(): pl.pallas_call(functools.partial(lattice_kernel, nb, cap, py), out_shape=...  2.36 us
    pallas_call x1, Pallas kernels, slot_call(): pl.pallas_call(functools.partial(slot_kernel, nb, cap), out_shape=[jax.Sh...  2.08 us
  transfers between devices with their start and end apart: 8, of which 3 were waited for; matrix products, arithmetic and copies ran while one was open for 8% of the time, Pallas kernels for 17%

profile of v1, /device:TPU:0, one launch (start us, length us, event | category | flops | bytes accessed | tf_op | source)
XLA Modules:
  0.0 51.0 jit_solution(7054015393421483303)
XLA Ops:
  0.7 1.1 %fusion.2 = (f32[5,16,8,128]{3,2,1,0:T(8,128)S(1)}, f32[5,16,8,128]{3,2,1,0:T(8,128)S(1)}) fusion(f32[5,64,8,128]{3,2,1,0:T(8,128)} %bitcast.30), kind=kLoop, calls=%fused_computation.8 | loop fusion | bytes 1310720 | tf_op jit(solution)/shard_map/slice | solution.py:641
  1.8 1.3 %collective-permute-start.1 = (f32[5,16,8,128]{3,2,1,0:T(8,128)S(1)}, f32[5,16,8,128]{3,2,1,0:T(8,128)S(1)}, u32[]{:S(2)}, u32[]{:S(2)}) collective-permute-start(f32[5,16,8,128]{3,2,1,0:T(8,128)S(1)} %get-tuple-element.40), channel_id=1, source_target_pairs={{4,0},{8,4},{12,8},{16,12},{20,16},{24,20},{28,24},{5,1},{9,5},{13... | collective-permute-start | bytes 983048 | tf_op jit(solution)/shard_map/ppermute | solution.py:624
  3.1 5.5 %collective-permute-start = (f32[5,16,8,128]{3,2,1,0:T(8,128)S(1)}, f32[5,16,8,128]{3,2,1,0:T(8,128)S(1)}, u32[]{:S(2)}, u32[]{:S(2)}) collective-permute-start(f32[5,16,8,128]{3,2,1,0:T(8,128)S(1)} %get-tuple-element.41), channel_id=1, source_target_pairs={{0,4},{4,8},{8,12},{12,16},{16,20},{20,24},{24,28},{1,5},{5,9},{9,... | collective-permute-start | bytes 983048 | tf_op jit(solution)/shard_map/ppermute | solution.py:624
  8.7 1.1 %fusion.1 = (f32[5,4,1,4,1,128]{5,4,3,2,1,0:T(1,128)S(1)}, f32[5,4,1,4,1,128]{5,4,3,2,1,0:T(1,128)S(1)}) fusion(f32[5,4,4,4,8,128]{5,4,3,2,1,0:T(8,128)} %bitcast.31), kind=kLoop, calls=%fused_computation.7 | loop fusion | bytes 163840 | tf_op jit(solution)/shard_map/slice | solution.py:645
  9.8 0.9 %collective-permute-start.2 = (f32[81,128]{1,0:T(8,128)S(1)}, f32[81,128]{1,0:T(8,128)S(1)}, u32[]{:S(2)}, u32[]{:S(2)}) collective-permute-start(f32[81,128]{1,0:T(8,128)S(1)} %pad_maximum_fusion), channel_id=1, source_target_pairs={{0,3},{1,0},{2,1},{3,2},{4,7},{5,4},{6,5},{7,6},{8,11},{9,8},{10,9... | collective-permute-start | bytes 124424 | tf_op jit(solution)/shard_map/ppermute | solution.py:629
  10.8 1.7 %collective-permute-done.2.yup_ref = f32[81,128]{1,0:T(8,128)S(1)} collective-permute-done((f32[81,128]{1,0:T(8,128)S(1)}, f32[81,128]{1,0:T(8,128)S(1)}, u32[]{:S(2)}, u32[]{:S(2)}) %collective-permute-start.2) | collective-permute-done | bytes 41504 | tf_op jit(solution)/shard_map/ppermute | solution.py:629
  12.5 1.3 %collective-permute-start.4 = (f32[9,128]{1,0:T(8,128)S(1)}, f32[9,128]{1,0:T(8,128)S(1)}, u32[]{:S(2)}, u32[]{:S(2)}) collective-permute-start(f32[9,128]{1,0:T(8,128)S(1)} %pad_maximum_fusion.1), channel_id=1, source_target_pairs={{4,0},{8,4},{12,8},{16,12},{20,16},{24,20},{28,24},{5,1},{9,5},{13... | collective-permute-start | bytes 13832 | tf_op jit(solution)/shard_map/ppermute | solution.py:624
  13.8 0.6 %copy.21 = f32[1,1,3,1024]{3,2,1,0:T(4,128)} copy(f32[1,1,3,1024]{3,1,2,0:T(1,128)S(1)} %copy-done.8) | data formatting | bytes 24576
  14.4 0.6 %copy.12.disp_ref = f32[3,2,9,128]{3,2,1,0:T(8,128)} copy(f32[3,2,9,128]{3,1,2,0:T(2,128)S(1)} %copy-done.7) | data formatting | bytes 55296 | tf_op args[2]
  15.0 0.6 %copy-done.5 = f32[80,128]{1,0:T(8,128)} copy-done((f32[80,128]{1,0:T(8,128)}, f32[80,128]{1,0:T(8,128)S(1)}, u32[]{:S(2)}) %copy-start.5) | copy-done | bytes 40984
  15.6 6.5 %volume.1 = (f32[5,64,8,128]{3,2,1,0:T(8,128)}, f32[2,3,2,8,128]{4,3,2,1,0:T(8,128)}) custom-call(f32[5,64,8,128]{3,2,1,0:T(8,128)} %bitcast.34, f32[5,64,8,128]{3,2,1,0:T(8,128)} %bitcast.32, f32[3,2,9,128]{3,2,1,0:T(8,128)} %copy.12.disp_ref, f32[81,128]{1,0:T(8,128)} %copy-done.1, f32[80,128]{1,0:T(8,128)} %copy-done.5), custom_call_target="tpu_custom_call" | custom-call | tf_op jit(solution)/shard_map/volume/pallas_call | solution.py:537
  22.1 0.6 %copy-done.6 = f32[9,128]{1,0:T(8,128)} copy-done((f32[9,128]{1,0:T(8,128)}, f32[9,128]{1,0:T(8,128)S(1)}, u32[]{:S(2)}) %copy-start.6) | copy-done | bytes 4632
  22.7 2.1 %slots.1 = (f32[24,128]{1,0:T(8,128)}, f32[96,128]{1,0:T(8,128)}) custom-call(f32[8,128]{1,0:T(8,128)} %bitcast.42, f32[81,128]{1,0:T(8,128)} %copy-done.1, f32[9,128]{1,0:T(8,128)} %copy-done.6, f32[3,1024]{1,0:T(4,128)} %bitcast.40), custom_call_target="tpu_custom_call" | custom-call | tf_op jit(solution)/shard_map/slots/pallas_call | solution.py:592
  24.8 0.7 %copy-done.2 = f32[5,16,8,128]{3,2,1,0:T(8,128)} copy-done((f32[5,16,8,128]{3,2,1,0:T(8,128)}, f32[5,16,8,128]{3,2,1,0:T(8,128)S(1)}, u32[]{:S(2)}) %copy-start.2) | copy-done | bytes 327704
  25.6 4.5 %faces.1 = (f32[5,64,8,128]{3,2,1,0:T(8,128)}, f32[256,128]{1,0:T(8,128)}, f32[2,3,8,128]{3,2,1,0:T(8,128)}, f32[6,128]{1,0:T(8,128)}) custom-call(f32[5,64,8,128]{3,2,1,0:T(8,128)} %bitcast.35, f32[5,64,8,128]{3,2,1,0:T(8,128)} %bitcast.33, f32[3,2,9,128]{3,2,1,0:T(8,128)} %copy.12.disp_ref, ...), custom_call_target="tpu_custom_call", output_to_operand_aliasing={{0}: (11, {})} | custom-call | tf_op jit(solution)/shard_map/faces/pallas_call | solution.py:570
  30.1 8.1 %all-to-all-start = ((f32[32,8,128]{2,1,0:T(8,128)}), f32[32,8,128]{2,1,0:T(8,128)S(1)}, u32[]{:S(2)}, u32[]{:S(2)}) async-start(f32[32,8,128]{2,1,0:T(8,128)} %bitcast.39), calls=%async_computation | async-start | bytes 262144 | tf_op jit(solution)/shard_map/all_to_all | solution.py:652
  38.5 0.7 %slice_bitcast_fusion = f32[3,8,128]{2,1,0:T(8,128)S(1)} fusion(f32[2,3,8,128]{3,2,1,0:T(8,128)} %get-tuple-element.31.part_ref), kind=kLoop, calls=%fused_computation.2 | loop fusion | bytes 24576 | tf_op jit(solution)/shard_map/squeeze | solution.py:654
  39.2 0.7 %copy.13 = f32[2,3,8,128]{3,1,2,0:T(4,128)S(1)} copy(f32[2,3,8,128]{3,2,1,0:T(8,128)} %get-tuple-element.31.part_ref) | data formatting | bytes 49152 | tf_op jit(solution)/shard_map/faces/pallas_call | solution.py:570
  40.0 1.5 %collective-permute-done.5.yrow_ref = f32[6,128]{1,0:T(8,128)S(1)} collective-permute-done((f32[6,128]{1,0:T(8,128)}, f32[6,128]{1,0:T(8,128)S(1)}, u32[]{:S(2)}, u32[]{:S(2)}) %collective-permute-start.5) | collective-permute-done | bytes 3104 | tf_op jit(solution)/shard_map/ppermute | solution.py:629
  41.6 3.7 %collective-permute-start.6 = (f32[3,8,128]{2,1,0:T(8,128)S(1)}, f32[3,8,128]{2,1,0:T(8,128)S(1)}, u32[]{:S(2)}, u32[]{:S(2)}) collective-permute-start(f32[3,8,128]{2,1,0:T(8,128)S(1)} %scatter-add.4), channel_id=1, source_target_pairs={{0,4},{4,8},{8,12},{12,16},{16,20},{20,24},{24,28},{1,5},{5,9},{9,... | collective-permute-start | bytes 36872 | tf_op jit(solution)/shard_map/ppermute | solution.py:624
  45.3 1.4 %collective-permute-done.6.xrow_ref = f32[3,8,128]{2,1,0:T(8,128)S(1)} collective-permute-done((f32[3,8,128]{2,1,0:T(8,128)S(1)}, f32[3,8,128]{2,1,0:T(8,128)S(1)}, u32[]{:S(2)}, u32[]{:S(2)}) %collective-permute-start.6) | collective-permute-done | bytes 12320 | tf_op jit(solution)/shard_map/ppermute | solution.py:624
  46.7 0.6 %copy-done.9 = f32[3,8,128]{2,1,0:T(8,128)} copy-done((f32[3,8,128]{2,1,0:T(8,128)}, f32[3,8,128]{2,1,0:T(8,128)S(1)}, u32[]{:S(2)}) %copy-start.9) | copy-done | bytes 12312
  47.3 2.4 %lattice.1 = (f32[3,8,128]{2,1,0:T(8,128)}, f32[3,864]{1,0:T(4,128)}) custom-call(f32[256,128]{1,0:T(8,128)} %bitcast.37, f32[2,3,8,128]{3,2,1,0:T(8,128)} %get-tuple-element.31.part_ref, f32[6,128]{1,0:T(8,128)} %copy-done.10, f32[3,8,128]{2,1,0:T(8,128)} %copy-done.9), custom_call_target="tpu_custom_call" | custom-call | tf_op jit(solution)/shard_map/lattice/pallas_call | solution.py:607
  49.7 1.3 %copy.16 = f32[1,1,3,864]{3,1,2,0:T(1,128)} copy(f32[1,1,3,864]{3,2,1,0:T(4,128)} %bitcast.45) | data formatting | bytes 20736
  (35 shorter events, 0.6 us)
Async XLA Ops:
  0.6 8.0 %copy-start.11 = (s32[1,1,1024,1]{2,3,1,0:T(1,128)S(1)}, s32[1,1,1024,1]{2,3,1,0:T(1,128)}, u32[]{:S(2)}) copy-start(s32[1,1,1024,1]{2,3,1,0:T(1,128)} %param.10) | copy-start | bytes 12292
  0.6 13.1 %copy-start.8 = (f32[1,1,3,1024]{3,1,2,0:T(1,128)S(1)}, f32[1,1,3,1024]{3,1,2,0:T(1,128)}, u32[]{:S(2)}) copy-start(f32[1,1,3,1024]{3,1,2,0:T(1,128)} %param.11) | copy-start | bytes 36868
  0.7 13.7 %copy-start.7 = (f32[3,2,9,128]{3,1,2,0:T(2,128)S(1)}, f32[3,2,9,128]{3,1,2,0:T(2,128)}, u32[]{:S(2)}) copy-start(f32[3,2,9,128]{3,1,2,0:T(2,128)} %param.9) | copy-start | bytes 82948
  1.8 23.0 %collective-permute-start.1 = (f32[5,16,8,128]{3,2,1,0:T(8,128)S(1)}, f32[5,16,8,128]{3,2,1,0:T(8,128)S(1)}, u32[]{:S(2)}, u32[]{:S(2)}) collective-permute-start(f32[5,16,8,128]{3,2,1,0:T(8,128)S(1)} %get-tuple-element.40), channel_id=1, source_target_pairs={{4,0},{8,4},{12,8},{16,12},{20,16},{24,20},{28,24},{5,1},{9,5},{13... | collective-permute-start | bytes 983048 | tf_op jit(solution)/shard_map/ppermute | solution.py:624
  3.1 21.7 %collective-permute-start = (f32[5,16,8,128]{3,2,1,0:T(8,128)S(1)}, f32[5,16,8,128]{3,2,1,0:T(8,128)S(1)}, u32[]{:S(2)}, u32[]{:S(2)}) collective-permute-start(f32[5,16,8,128]{3,2,1,0:T(8,128)S(1)} %get-tuple-element.41), channel_id=1, source_target_pairs={{0,4},{4,8},{8,12},{12,16},{16,20},{20,24},{24,28},{1,5},{5,9},{9,... | collective-permute-start | bytes 983048 | tf_op jit(solution)/shard_map/ppermute | solution.py:624
  8.7 13.4 %copy-start.4 = (f32[1,1,1024,1]{2,3,1,0:T(1,128)}, f32[1,1,1024,1]{2,3,1,0:T(1,128)S(1)}, u32[]{:S(2)}) copy-start(f32[1,1,1024,1]{2,3,1,0:T(1,128)S(1)} %convert_element_type.5) | copy-start | bytes 12292
  9.8 2.6 %collective-permute-start.2 = (f32[81,128]{1,0:T(8,128)S(1)}, f32[81,128]{1,0:T(8,128)S(1)}, u32[]{:S(2)}, u32[]{:S(2)}) collective-permute-start(f32[81,128]{1,0:T(8,128)S(1)} %pad_maximum_fusion), channel_id=1, source_target_pairs={{0,3},{1,0},{2,1},{3,2},{4,7},{5,4},{6,5},{7,6},{8,11},{9,8},{10,9... | collective-permute-start | bytes 124424 | tf_op jit(solution)/shard_map/ppermute | solution.py:629
  10.8 4.3 %collective-permute-start.3 = (f32[80,128]{1,0:T(8,128)S(1)}, f32[80,128]{1,0:T(8,128)S(1)}, u32[]{:S(2)}, u32[]{:S(2)}) collective-permute-start(f32[80,128]{1,0:T(8,128)S(1)} %bitcast.44), channel_id=1, source_target_pairs={{0,1},{1,2},{2,3},{3,0},{4,5},{5,6},{6,7},{7,4},{8,9},{9,10},{10,1... | collective-permute-start | bytes 122888 | tf_op jit(solution)/shard_map/ppermute | solution.py:629
  12.5 2.6 %copy-start.1 = (f32[81,128]{1,0:T(8,128)}, f32[81,128]{1,0:T(8,128)S(1)}, u32[]{:S(2)}) copy-start(f32[81,128]{1,0:T(8,128)S(1)} %collective-permute-done.2.yup_ref) | copy-start | bytes 124420
  12.5 9.6 %collective-permute-start.4 = (f32[9,128]{1,0:T(8,128)S(1)}, f32[9,128]{1,0:T(8,128)S(1)}, u32[]{:S(2)}, u32[]{:S(2)}) collective-permute-start(f32[9,128]{1,0:T(8,128)S(1)} %pad_maximum_fusion.1), channel_id=1, source_target_pairs={{4,0},{8,4},{12,8},{16,12},{20,16},{24,20},{28,24},{5,1},{9,5},{13... | collective-permute-start | bytes 13832 | tf_op jit(solution)/shard_map/ppermute | solution.py:624
  15.0 0.6 %copy-start.5 = (f32[80,128]{1,0:T(8,128)}, f32[80,128]{1,0:T(8,128)S(1)}, u32[]{:S(2)}) copy-start(f32[80,128]{1,0:T(8,128)S(1)} %collective-permute-done.3.ydn_ref) | copy-start | bytes 122884
  22.1 0.6 %copy-start.6 = (f32[9,128]{1,0:T(8,128)}, f32[9,128]{1,0:T(8,128)S(1)}, u32[]{:S(2)}) copy-start(f32[9,128]{1,0:T(8,128)S(1)} %collective-permute-done.4.far_ref) | copy-start | bytes 13828
  24.8 0.7 %copy-start.2 = (f32[5,16,8,128]{3,2,1,0:T(8,128)}, f32[5,16,8,128]{3,2,1,0:T(8,128)S(1)}, u32[]{:S(2)}) copy-start(f32[5,16,8,128]{3,2,1,0:T(8,128)S(1)} %collective-permute-done.1.upper_ref) | copy-start | bytes 983044
  24.8 0.8 %copy-start.3 = (f32[5,16,8,128]{3,2,1,0:T(8,128)}, f32[5,16,8,128]{3,2,1,0:T(8,128)S(1)}, u32[]{:S(2)}) copy-start(f32[5,16,8,128]{3,2,1,0:T(8,128)S(1)} %collective-permute-done.lower_ref) | copy-start | bytes 983044
  30.1 16.6 %all-to-all-start = ((f32[32,8,128]{2,1,0:T(8,128)}), f32[32,8,128]{2,1,0:T(8,128)S(1)}, u32[]{:S(2)}, u32[]{:S(2)}) async-start(f32[32,8,128]{2,1,0:T(8,128)} %bitcast.39), calls=%async_computation | async-start | bytes 262144 | tf_op jit(solution)/shard_map/all_to_all | solution.py:652
  38.2 3.3 %collective-permute-start.5 = (f32[6,128]{1,0:T(8,128)}, f32[6,128]{1,0:T(8,128)S(1)}, u32[]{:S(2)}, u32[]{:S(2)}) collective-permute-start(f32[6,128]{1,0:T(8,128)} %get-tuple-element.32), channel_id=1, source_target_pairs={{0,1},{1,2},{2,3},{3,0},{4,5},{5,6},{6,7},{7,4},{8,9},{9,10},{10,1... | collective-permute-start | bytes 9224 | tf_op jit(solution)/shard_map/ppermute | solution.py:629
  41.5 5.2 %copy-start.10 = (f32[6,128]{1,0:T(8,128)}, f32[6,128]{1,0:T(8,128)S(1)}, u32[]{:S(2)}) copy-start(f32[6,128]{1,0:T(8,128)S(1)} %collective-permute-done.5.yrow_ref) | copy-start | bytes 9220
  41.6 5.1 %collective-permute-start.6 = (f32[3,8,128]{2,1,0:T(8,128)S(1)}, f32[3,8,128]{2,1,0:T(8,128)S(1)}, u32[]{:S(2)}, u32[]{:S(2)}) collective-permute-start(f32[3,8,128]{2,1,0:T(8,128)S(1)} %scatter-add.4), channel_id=1, source_target_pairs={{0,4},{4,8},{8,12},{12,16},{16,20},{20,24},{24,28},{1,5},{5,9},{9,... | collective-permute-start | bytes 36872 | tf_op jit(solution)/shard_map/ppermute | solution.py:624
  46.7 0.6 %copy-start.9 = (f32[3,8,128]{2,1,0:T(8,128)}, f32[3,8,128]{2,1,0:T(8,128)S(1)}, u32[]{:S(2)}) copy-start(f32[3,8,128]{2,1,0:T(8,128)S(1)} %collective-permute-done.6.xrow_ref) | copy-start | bytes 36868
  46.7 0.7 %copy-start = (f32[32,8,128]{2,1,0:T(8,128)}, f32[32,8,128]{2,1,0:T(8,128)S(1)}, u32[]{:S(2)}) copy-start(f32[32,8,128]{2,1,0:T(8,128)S(1)} %all-to-all-done) | copy-start | bytes 393220

commit v2 on v1

v2 whole, which is shorter than its diff:
```python
import functools
import math

import jax
import jax.numpy as jnp
import numpy as np
from jax import lax
from jax.experimental import pallas as pl
from jax.experimental.pallas import tpu as pltpu
from jax.sharding import PartitionSpec as P

LU = 12
LV = 12
LW = 6
F32 = jnp.float32
POINTS = [-1.0, -1.0 / math.sqrt(5.0), 1.0 / math.sqrt(5.0), 1.0]
WEIGHTS = [1.0 / 6.0, 5.0 / 6.0, 5.0 / 6.0, 1.0 / 6.0]
UPPER = [0.5 * (1.0 + point) for point in POINTS]


def derivative_matrix():
    matrix = np.zeros((4, 4))
    for target in range(4):
        for source in range(4):
            others = [m for m in range(4) if m != source]
            if target == source:
                matrix[target, source] = sum(1.0 / (POINTS[source] - POINTS[m]) for m in others)
            else:
                upper = np.prod([POINTS[target] - POINTS[m] for m in others if m != target])
                lower = np.prod([POINTS[source] - POINTS[m] for m in others])
                matrix[target, source] = upper / lower
    return matrix


DM = derivative_matrix()


def line_slopes(line, scale):
    e0 = line[0] + line[3]
    o0 = line[0] - line[3]
    e1 = line[1] + line[2]
    o1 = line[1] - line[2]
    even = e0 - e1
    out = [None] * 4
    for m in range(2):
        half = 0.5 * scale[m]
        p0 = float(half * (DM[m, 0] - DM[m, 3]))
        p1 = float(half * (DM[m, 1] - DM[m, 2]))
        k = float(half * (DM[m, 0] + DM[m, 3]))
        odd_part = p0 * o0 + p1 * o1
        even_part = k * even
        out[m] = odd_part + even_part
        out[3 - m] = odd_part - even_part
    return out


def spread(low, high):
    step = high - low
    return [low, low + float(UPPER[1]) * step, low + float(UPPER[2]) * step, high]


def gather_back(g):
    middle = float(UPPER[1]) * g[1] + float(UPPER[2]) * g[2]
    return (g[0] + g[1] + g[2] - middle, g[3] + middle)


def cross(x, y):
    return [x[1] * y[2] - x[2] * y[1], x[2] * y[0] - x[0] * y[2], x[0] * y[1] - x[1] * y[0]]


def dot3(x, y):
    return x[0] * y[0] + x[1] * y[1] + x[2] * y[2]


def add(x, y):
    return y if x is None else x + y


def add3(x, y):
    return y if x is None else [x[i] + y[i] for i in range(3)]


def primitives(u):
    inverse = 1.0 / u[0]
    v = [u[1] * inverse, u[2] * inverse, u[3] * inverse]
    mv = u[1] * v[0] + u[2] * v[1] + u[3] * v[2]
    p = 0.4 * u[4] - 0.2 * mv
    return inverse, v, mv * inverse, p, u[4] + p


class Node:
    def __init__(self, u):
        self.inverse, self.v, self.v2, self.p, self.ep = primitives(u)
        self.big = [u[0], u[1], u[2], u[3], self.ep]
        self.w = [None] * 5
        self.pb = None
        self.b = None

    def work(self, s):
        return sum((s[f] * self.big[f] for f in range(1, 5)), s[0] * self.big[0])

    def volume(self, adj, s, vn):
        back = []
        for d in range(3):
            k = self.work(s[d])
            for f in range(5):
                self.w[f] = add(self.w[f], vn[d] * s[d][f])
            self.pb = add(self.pb, dot3(adj[d], s[d][1:4]))
            self.b = add3(self.b, [adj[d][c] * k for c in range(3)])
            back.append([self.v[c] * k + self.p * s[d][1 + c] for c in range(3)])
        self.pb = self.pb + self.w[4]
        return back

    def face(self, n, vn, jump, sigma):
        k = self.work(jump)
        square = dot3(n, n)
        root = lax.rsqrt(square)
        twice = 2.0 * root
        length = twice * square
        if isinstance(sigma, int) and sigma == 1:
            cf = vn + length
        elif isinstance(sigma, int):
            cf = vn - length
            twice = -twice
        else:
            cf = vn + sigma * length
            twice = sigma * twice
        q = k - jump[4] * self.p
        along = twice * q
        for f in range(5):
            self.w[f] = add(self.w[f], cf * jump[f])
        self.pb = add(self.pb, dot3(n, jump[1:4]) + vn * jump[4])
        self.b = add3(self.b, [n[c] * k for c in range(3)])
        return [self.v[c] * k + self.p * jump[1 + c] + n[c] * along for c in range(3)]

    def gradient(self):
        pb4 = 0.4 * self.pb
        rb = [self.b[c] * self.inverse for c in range(3)]
        out = [self.w[0] - dot3(self.v, rb) + (0.5 * pb4) * self.v2]
        for c in range(3):
            out.append(self.w[1 + c] + rb[c] - pb4 * self.v[c])
        out.append(self.w[4] + pb4)
        return out


def corner(disp_ref, c, e1, e2):
    return disp_ref[pl.ds(9 * c + e2, 8), e1, :]


def with_next(window):
    return [window, pltpu.roll(window, 127, 1)]


def trace_kernel(lam_ref, cube_ref, blk_ref, coords_ref, disp_ref, own_even, own_odd, y_even, y_odd, blkf, coords, disp, tiles, blocks, sem):
    x_odd = lax.axis_index("px") % 2
    y_up = 1 - lax.axis_index("py") % 2
    copies = [
        pltpu.make_async_copy(lam_ref.at[:, pl.ds(48 - 48 * x_odd, 16)], own_even, sem.at[0]),
        pltpu.make_async_copy(lam_ref.at[:, pl.ds(48 * x_odd, 16)], own_odd, sem.at[1]),
        pltpu.make_async_copy(cube_ref.at[:, :, 0], tiles.at[0], sem.at[2]),
        pltpu.make_async_copy(cube_ref.at[:, :, 3], tiles.at[1], sem.at[3]),
        pltpu.make_async_copy(blk_ref, blocks, sem.at[4]),
        pltpu.make_async_copy(coords_ref, coords, sem.at[5]),
        pltpu.make_async_copy(disp_ref, disp, sem.at[6]),
    ]
    for copy in copies:
        copy.start()
    for copy in copies[2:5]:
        copy.wait()
    blkf[...] = blocks[...].astype(F32)
    rows = tiles.reshape(1280, 128)
    bottom = rows[pl.ds(0, 80, stride=8), :]
    top = rows[pl.ds(640 + 7, 80, stride=8), :]
    y_even[0:80, :] = jnp.where(y_up == 1, top, bottom)
    y_odd[0:80, :] = jnp.where(y_up == 1, bottom, top)
    first_row = blocks[0:1, :].astype(F32)
    y_even[80:81, :] = first_row
    y_odd[80:81, :] = first_row
    for copy in copies[:2] + copies[5:]:
        copy.wait()


def volume_kernel(u_ref, lam_ref, disp_ref, even_ref, odd_ref, grad_ref, ukeep, gkeep, cols, g_ref, lam, umid, gmid, j0t, j1t, j2t, j0b, j1b, j2b, s1, s2, yj, sem):
    lam_copies = [pltpu.make_async_copy(lam_ref.at[f], lam.at[f], sem.at[f]) for f in range(5)]
    u_at = [ukeep.at[0], umid.at[0], umid.at[1], ukeep.at[1]]
    g_at = [gkeep.at[0], gmid.at[0], gmid.at[1], gkeep.at[1]]
    u_copies = [pltpu.make_async_copy(u_ref.at[:, pl.ds(16 * a, 16)], u_at[a], sem.at[5 + a]) for a in range(4)]
    for copy in lam_copies + u_copies:
        copy.start()

    for c in range(3):
        x = [[with_next(corner(disp_ref, c, e1, e2)) for e2 in range(2)] for e1 in range(2)]
        for d in range(3):
            ends = []
            for i in range(2):
                pair = []
                for j in range(2):
                    low = [(0, i, j), (i, 0, j), (i, j, 0)][d]
                    high = [(1, i, j), (i, 1, j), (i, j, 1)][d]
                    half = 0.5 * (x[high[0]][high[1]][high[2]] - x[low[0]][low[1]][low[2]])
                    pair.append(half + 0.5 if c == d else half)
                ends.append(spread(pair[0], pair[1]))
            for j in range(4):
                values = spread(ends[0][j], ends[1][j])
                for i in range(4):
                    [j0t, j1t, j2t][d][i, j, c] = values[i]
                    if d and i in (0, 3):
                        cols[i // 3, d - 1, j, c] = values[i]
    for f in range(5):
        lam_copies[f].wait()
        for b in range(4):
            for c in range(4):
                line = [lam[f, 16 * i + 4 * b + c] for i in range(4)]
                out = line_slopes(line, [-WEIGHTS[i] * WEIGHTS[b] * WEIGHTS[c] for i in range(4)])
                for i in range(4):
                    s1[i, 4 * b + c, f] = out[i]

    above_even = lax.axis_index("py") % 2 == 0
    rows = lax.broadcasted_iota(jnp.int32, (8, 128), 0)
    first_row = rows == 0
    last_row = rows == 7
    mid_copies = []
    for a in range(4):
        base = 16 * a
        wa = WEIGHTS[a]
        u_copies[a].wait()
        for f in range(5):
            for c in range(4):
                line = [lam[f, base + 4 * b + c] for b in range(4)]
                out = line_slopes(line, [-wa * WEIGHTS[b] * WEIGHTS[c] for b in range(4)])
                for b in range(4):
                    s2[4 * b + c, f] = out[b]
                half = float(0.5 * wa * WEIGHTS[c])
                at = f * 16 + a * 4 + c
                one = jnp.broadcast_to(even_ref[at : at + 1, :], TILE)
                two = jnp.broadcast_to(odd_ref[at : at + 1, :], TILE)
                above = jnp.where(above_even, one, two)
                below = jnp.where(above_even, two, one)
                plus = jnp.where(last_row, above, pltpu.roll(line[0], 7, 0))
                top = half * (line[3] - plus)
                bottom = half * (below - line[0])
                yj[1, c, f] = top
                yj[0, c, f] = jnp.where(first_row, bottom, pltpu.roll(top, 1, 0))
        for b in range(4):
            slopes3 = []
            ztop = []
            zbot = []
            half = float(0.5 * wa * WEIGHTS[b])
            for f in range(5):
                line = [lam[f, base + 4 * b + c] for c in range(4)]
                slopes3.append(line_slopes(line, [-wa * WEIGHTS[b] * WEIGHTS[c] for c in range(4)]))
                top = half * (line[3] - pltpu.roll(line[0], 127, 1))
                ztop.append(top)
                zbot.append(pltpu.roll(top, 1, 1))
            back2 = None
            col2 = [j2t[a, b, k] for k in range(3)]
            for c in range(4):
                n = 4 * b + c
                node = Node([u_at[a][f, n] for f in range(5)])
                col0 = [j0t[b, c, k] for k in range(3)]
                col1 = [j1t[a, c, k] for k in range(3)]
                adj = [cross(col1, col2), cross(col2, col0), cross(col0, col1)]
                s = [[s1[a, n, f] for f in range(5)], [s2[n, f] for f in range(5)], [slopes3[f][c] for f in range(5)]]
                vn = [dot3(adj[d], node.v) for d in range(3)]
                back = node.volume(adj, s, vn)
                if b == 0:
                    back[1] = add3(back[1], node.face(adj[1], vn[1], [yj[0, c, f] for f in range(5)], -1))
                if b == 3:
                    back[1] = add3(back[1], node.face(adj[1], vn[1], [yj[1, c, f] for f in range(5)], 1))
                if c == 0:
                    back[2] = add3(back[2], node.face(adj[2], vn[2], zbot, -1))
                if c == 3:
                    back[2] = add3(back[2], node.face(adj[2], vn[2], ztop, 1))
                grads = node.gradient()
                for f in range(5):
                    g_at[a][f, n] = grads[f]
                back0 = add3(cross(back[1], col2), cross(col1, back[2]))
                back1 = add3(cross(col2, back[0]), cross(back[2], col0))
                back2 = add3(back2, add3(cross(back[0], col1), cross(col0, back[1])))
                for k in range(3):
                    j0b[b, c, k] = back0[k] if a == 0 else j0b[b, c, k] + back0[k]
                    j1b[a, c, k] = back1[k] if b == 0 else j1b[a, c, k] + back1[k]
            for k in range(3):
                j2b[a, b, k] = back2[k]
        if a in (1, 2):
            copy = pltpu.make_async_copy(gmid.at[a - 1], grad_ref.at[:, pl.ds(base, 16)], sem.at[8 + a])
            copy.start()
            mid_copies.append(copy)

    for c in range(3):
        gx = [[[None, None], [None, None]], [[None, None], [None, None]]]
        for d in range(3):
            table = [j0b, j1b, j2b][d]
            ends = [[], []]
            for i in range(4):
                low, high = gather_back([table[i, j, c] for j in range(4)])
                ends[0].append(low)
                ends[1].append(high)
            for j in range(2):
                pair = gather_back(ends[j])
                for i in range(2):
                    half = 0.5 * pair[i]
                    low = [(0, i, j), (i, 0, j), (i, j, 0)][d]
                    high = [(1, i, j), (i, 1, j), (i, j, 1)][d]
                    gx[high[0]][high[1]][high[2]] = add(gx[high[0]][high[1]][high[2]], half)
                    gx[low[0]][low[1]][low[2]] = add(gx[low[0]][low[1]][low[2]], -half)
        for e1 in range(2):
            for e2 in range(2):
                g_ref[e1, c, e2] = gx[e1][e2][0] + pltpu.roll(gx[e1][e2][1], 1, 1)
    for copy in mid_copies:
        copy.wait()


def one_side(side, scale, sigma, wall, u_ref, own_ref, received_ref, gkeep, cols, g_ref, grad_ref, part_ref, row_ref, gout, sem):
    col1 = [[cols[side, 0, c, k] for k in range(3)] for c in range(4)]
    back1 = [None] * 4
    back2 = [None] * 4
    for b in range(4):
        col2 = [cols[side, 1, b, k] for k in range(3)]
        for c in range(4):
            n = 4 * b + c
            weight = float(WEIGHTS[b] * WEIGHTS[c])
            u = [u_ref[side, f, n] for f in range(5)]
            own = [own_ref[f, n] for f in range(5)]
            normal = cross(col1[c], col2)
            if wall:
                inverse, v, v2, p, ep = primitives(u)
                vn = dot3(normal, v)
                m = u[1:4]
                jump = [-weight * own[f] for f in range(1, 4)]
                square = dot3(normal, normal)
                root = lax.rsqrt(square)
                rate = vn * (root * root)
                q = u[0] * vn
                level = dot3(jump, normal)
                slope = 2.0 * (rate - root)
                phi = q * (rate - 2.0 * root) + p
                lk = level * slope
                along = lk * q * (root * root)
                grads = [level * (0.2 * v2 - rate * vn)]
                for k in range(3):
                    grads.append(lk * normal[k] - (0.4 * level) * v[k])
                grads.append(0.4 * level)
                back = [jump[k] * phi + lk * m[k] - along * normal[k] for k in range(3)]
            else:
                node = Node(u)
                vn = dot3(normal, node.v)
                factor = scale * weight
                jump = [factor * (own[f] - received_ref[f, n]) for f in range(5)]
                back = node.face(normal, vn, jump, sigma)
                grads = node.gradient()
            for f in range(5):
                gout[f, n] = gkeep[side, f, n] + grads[f]
            back1[c] = add3(back1[c], cross(col2, back))
            back2[b] = add3(back2[b], cross(back, col1[c]))
        pltpu.make_async_copy(
            gout.at[:, pl.ds(4 * b, 4)], grad_ref.at[:, pl.ds(48 * side + 4 * b, 4)], sem.at[b]
        ).start()
    rows = lax.broadcasted_iota(jnp.int32, TILE, 0)
    for k in range(3):
        low1, high1 = gather_back([back1[i][k] for i in range(4)])
        low2, high2 = gather_back([back2[i][k] for i in range(4)])
        gx = [[-0.5 * (low1 + low2), 0.5 * (low2 - high1)], [0.5 * (low1 - high2), 0.5 * (high1 + high2)]]
        near = g_ref[side, k, 0] + gx[0][0] + pltpu.roll(gx[0][1], 1, 1)
        far = g_ref[side, k, 1] + gx[1][0] + pltpu.roll(gx[1][1], 1, 1)
        part_ref[side, k] = near + jnp.where(rows == 0, 0.0, pltpu.roll(far, 1, 0))
        row_ref[pl.ds(3 * side + k, 1), :] = far[7:8, :]


def wait_side(side, grad_ref, gout, sem):
    for b in range(4):
        pltpu.make_async_copy(
            gout.at[:, pl.ds(4 * b, 4)], grad_ref.at[:, pl.ds(48 * side + 4 * b, 4)], sem.at[b]
        ).wait()


def block_ranks(nb, groups, emit):
    block_of = lax.broadcasted_iota(jnp.int32, (nb, 128), 0).astype(F32)
    k_of = lax.broadcasted_iota(jnp.int32, (128, 256), 0)
    z_of = lax.broadcasted_iota(jnp.int32, (128, 256), 1)
    before = jnp.where((k_of < z_of) | (z_of >= 128), 1.0, 0.0).astype(jnp.bfloat16)
    here = [jnp.where(jnp.broadcast_to(row, (nb, 128)) == block_of, 1.0, 0.0) for row in sum(groups, [])]
    counts = jnp.dot(
        jnp.concatenate(here, axis=0).astype(jnp.bfloat16), before, preferred_element_type=F32
    )
    i = 0
    for group in groups:
        offset = None
        for _ in group:
            mine = counts[nb * i : nb * (i + 1)]
            earlier = mine[:, 0:128] if offset is None else mine[:, 0:128] + offset
            emit(i, here[i], jnp.sum(here[i] * earlier, axis=0, keepdims=True))
            offset = add(offset, mine[:, 128:256])
            i += 1


def first_face_kernel(grad_in_ref, u_ref, own_ref, received_ref, gkeep, cols, g_ref, grad_ref, part_ref, row_ref, gout, sem):
    side = 1 - lax.axis_index("px") % 2
    sign = jnp.where(side == 0, F32(-1.0), F32(1.0))
    one_side(side, 0.5 * sign, sign, False, u_ref, own_ref, received_ref, gkeep, cols, g_ref, grad_ref, part_ref, row_ref, gout, sem)
    wait_side(side, grad_ref, gout, sem)


def label_kernel(nb, even_ref, odd_ref, far_ref, row_ref, label_ref):
    beside = jnp.where(lax.axis_index("py") % 2 == 0, even_ref[80:81, :], odd_ref[80:81, :])
    across = far_ref[8:9, :]
    label_ref[0:8, :] = far_ref[0:8, :]
    label_ref[8:9, :] = beside
    label_ref[9:10, :] = across

    def emit(i, here, rank):
        label_ref[16 + i : 17 + i, :] = rank

    block_ranks(nb, [[far_ref[y : y + 1, :] for y in range(8)], [beside], [across]], emit)


def second_face_kernel(nb, cap, px, grad_in_ref, u_ref, own_ref, received_ref, gkeep, cols, g_ref, part_in_ref, row_in_ref, mine_ref, label_ref, cpack_ref, grad_ref, buf_ref, part_ref, row_ref, gout, lhs, rhs, sem):
    index = lax.axis_index("px")
    side = index % 2
    is_first = index == 0
    is_last = index == px - 1
    part_ref[1 - side] = part_in_ref[1 - side]
    row_ref[...] = row_in_ref[...]
    rest = (u_ref, own_ref, received_ref, gkeep, cols, g_ref, grad_ref, part_ref, row_ref, gout, sem)

    @pl.when(is_first)
    def _():
        one_side(side, None, None, True, *rest)

    @pl.when(jnp.logical_not(is_first))
    def _():
        scale = jnp.where(side == 0, F32(-0.5), jnp.where(is_last, F32(1.0), F32(0.5)))
        sigma = jnp.where(side == 0, F32(-1.0), jnp.where(is_last, F32(0.0), F32(1.0)))
        one_side(side, scale, sigma, False, *rest)

    block_of = lax.broadcasted_iota(jnp.int32, (nb, 128), 0).astype(F32)
    slot_of = (lax.broadcasted_iota(jnp.int32, (128, 128), 0) & (cap - 1)).astype(F32)
    sums = []
    for stream, count in enumerate((8, 8, 1, 1)):
        for y in range(count):
            block, values, rank = [
                (mine_ref[y : y + 1, :], lambda k: part_ref[0, k, y : y + 1, :], mine_ref[8 + y : 9 + y, :]),
                (label_ref[y : y + 1, :], lambda k: part_ref[1, k, y : y + 1, :], label_ref[16 + y : 17 + y, :]),
                (label_ref[8:9, :], lambda k: row_ref[k : k + 1, :], label_ref[24:25, :]),
                (label_ref[9:10, :], lambda k: row_ref[3 + k : 4 + k, :], label_ref[25:26, :]),
            ][stream]
            lanes = pl.ds(128 * y, 128)
            here = jnp.broadcast_to(block, (nb, 128)) == block_of
            rhs[:, lanes] = jnp.where(jnp.broadcast_to(rank, (128, 128)) == slot_of, 1.0, 0.0).astype(jnp.bfloat16)
            for k in range(3):
                row = values(k)
                high = row.astype(jnp.bfloat16).astype(F32)
                for part, piece in enumerate((high, row - high)):
                    lhs[pl.ds((3 * part + k) * nb, nb), lanes] = jnp.where(
                        here, jnp.broadcast_to(piece, (nb, 128)), 0.0
                    ).astype(jnp.bfloat16)
        total = lax.dot_general(
            lhs[:, pl.ds(0, 128 * count)],
            rhs[:, pl.ds(0, 128 * count)],
            (((1,), (1,)), ((), ())),
            preferred_element_type=F32,
        )
        total = total[0 : 3 * nb] + total[3 * nb : 6 * nb]
        sums.append([total[k * nb : (k + 1) * nb] for k in range(3)])
    items = [sums[stream][k] for k in range(3) for stream in range(4)]
    items += [cpack_ref[pl.ds(k * nb, nb), :] for k in range(3)]
    per_row = 128 // cap
    height = buf_ref.shape[0] // nb
    position = lax.broadcasted_iota(jnp.int32, (nb, 128), 1) // cap
    for r in range(height):
        inside = items[r * per_row : (r + 1) * per_row]
        value = inside[0]
        for i, item in enumerate(inside[1:], 1):
            value = jnp.where(position == i, item, value)
        buf_ref[pl.ds(r, nb, stride=height), :] = value
    wait_side(side, grad_ref, gout, sem)


def slot_kernel(nb, cap, blk_ref, coords_ref, mine_ref, cpack_ref, lhs, rhs):
    mine_ref[0:8, :] = blk_ref[...]
    slot_of = (lax.broadcasted_iota(jnp.int32, (128, 128), 0) & (cap - 1)).astype(F32)

    def emit(y, here, rank):
        mine_ref[8 + y : 9 + y, :] = rank
        lanes = pl.ds(128 * y, 128)
        rhs[:, lanes] = jnp.where(jnp.broadcast_to(rank, (128, 128)) == slot_of, 1.0, 0.0).astype(jnp.bfloat16)
        for k in range(3):
            rest = coords_ref[k, y : y + 1, :]
            for part in range(3):
                piece = rest.astype(jnp.bfloat16).astype(F32)
                rest = rest - piece
                lhs[pl.ds((3 * part + k) * nb, nb), lanes] = (
                    here * jnp.broadcast_to(piece, (nb, 128))
                ).astype(jnp.bfloat16)

    block_ranks(nb, [[blk_ref[y : y + 1, :] for y in range(8)]], emit)
    total = lax.dot_general(lhs[...], rhs[...], (((1,), (1,)), ((), ())), preferred_element_type=F32)
    cpack_ref[...] = total[0 : 3 * nb] + total[3 * nb : 6 * nb] + total[6 * nb : 9 * nb]


def powers(t, degree):
    out = [None, t]
    for n in range(2, degree + 1):
        out.append(out[n // 2] * out[n - n // 2])
    return out


def bernstein(t, degree):
    up = powers(t, degree)
    down = powers(1.0 - t, degree)
    out = []
    for a in range(degree + 1):
        if a == 0:
            out.append(down[degree])
        elif a == degree:
            out.append(up[degree])
        else:
            out.append(float(math.comb(degree, a)) * up[a] * down[degree - a])
    return out


def lattice_kernel(nb, cap, py, buf_ref, part_ref, yrow_ref, xrow_ref, owned_ref, out_ref, lhs, rhs):
    rows = lax.broadcasted_iota(jnp.int32, TILE, 0)
    for k in range(3):
        beside = jnp.broadcast_to(yrow_ref[k : k + 1, :], TILE)
        owned_ref[k] = part_ref[0, k] + jnp.where(rows == 0, beside, 0.0) + xrow_ref[k]
    per_row = 128 // cap
    height = buf_ref.shape[0] // nb
    source = lax.broadcasted_iota(jnp.int32, (nb, 128), 0)
    lane = lax.broadcasted_iota(jnp.int32, (16, 128), 1)

    def item(j):
        value = buf_ref[pl.ds(j // per_row, nb, stride=height), :]
        at = j % per_row
        return pltpu.roll(value, 128 - at * cap, 1) if at else value

    def from_px(value):
        return jnp.where(source >= py, pltpu.roll(value, py, 0), 0.0)

    def from_py(value):
        return jnp.where(source % py > 0, pltpu.roll(value, 1, 0), pltpu.roll(value, nb - (py - 1), 0))

    def dense(value):
        out = value[0:16]
        for i in range(1, per_row):
            piece = pltpu.roll(value[16 * i : 16 * (i + 1)], i * cap, 1)
            out = jnp.where(lane // cap == i, piece, out)
        return out

    sens = []
    for k in range(3):
        own, above, beside, across = [item(4 * k + stream) for stream in range(4)]
        sens.append(dense(own + from_py(beside) + from_px(above + from_py(across))))
    u, v, w = [dense(item(12 + k)) for k in range(3)]
    bu = bernstein(u, LU - 1)
    bv = bernstein(v, LV - 1)
    bw = bernstein(w, LW - 1)
    for a in range(LU):
        for k in range(3):
            lhs[pl.ds(16 * (3 * a + k), 16), :] = sens[k] * bu[a]
    for b in range(LV):
        for c in range(LW):
            rhs[pl.ds(16 * (LW * b + c), 16), :] = bv[b] * bw[c]
    left = jnp.concatenate([lhs[pl.ds(i, 3 * LU, stride=16), :] for i in range(16)], axis=1)
    right = jnp.concatenate([rhs[pl.ds(i, LV * LW, stride=16), :] for i in range(16)], axis=1)
    left_high = left.astype(jnp.bfloat16)
    left_low = (left - left_high.astype(F32)).astype(jnp.bfloat16)
    right_high = right.astype(jnp.bfloat16)
    right_low = (right - right_high.astype(F32)).astype(jnp.bfloat16)

    def product(x, y):
        return lax.dot_general(x, y, (((1,), (1,)), ((), ())), preferred_element_type=F32)

    total = product(left_high, right_high) + (product(left_high, right_low) + product(left_low, right_high))
    for a in range(LU):
        for k in range(3):
            out_ref[k, :, pl.ds(LV * LW * a, LV * LW)] = total[3 * a + k : 3 * a + k + 1, :]


TILE = (8, 128)
VMEM = pl.BlockSpec(memory_space=pltpu.VMEM)
HBM = pl.BlockSpec(memory_space=pltpu.HBM)


def near(*arrays):
    return [pltpu.with_memory_space_constraint(array, pltpu.VMEM) for array in arrays]


def volume_call(u, lam, disp, even, odd):
    return pl.pallas_call(
        volume_kernel,
        in_specs=[HBM, HBM, VMEM, VMEM, VMEM],
        out_specs=[HBM, VMEM, VMEM, VMEM, VMEM],
        out_shape=[
            jax.ShapeDtypeStruct((5, 64) + TILE, F32),
            pltpu.VMEM((2, 5, 16) + TILE, F32),
            pltpu.VMEM((2, 5, 16) + TILE, F32),
            pltpu.VMEM((2, 2, 4, 3) + TILE, F32),
            pltpu.VMEM((2, 3, 2) + TILE, F32),
        ],
        scratch_shapes=[
            pltpu.VMEM((5, 64) + TILE, F32),
            pltpu.VMEM((2, 5, 16) + TILE, F32),
            pltpu.VMEM((2, 5, 16) + TILE, F32),
        ]
        + [pltpu.VMEM((4, 4, 3) + TILE, F32)] * 6
        + [
            pltpu.VMEM((4, 16, 5) + TILE, F32),
            pltpu.VMEM((16, 5) + TILE, F32),
            pltpu.VMEM((2, 4, 5) + TILE, F32),
            pltpu.SemaphoreType.DMA((11,)),
        ],
        name="volume",
    )(u, lam, *near(disp, even, odd))


def trace_call(lam, cube, blk, coords, disp):
    return pl.pallas_call(
        trace_kernel,
        in_specs=[HBM] * 5,
        out_specs=[VMEM] * 7,
        out_shape=[
            pltpu.VMEM((5, 16) + TILE, F32),
            pltpu.VMEM((5, 16) + TILE, F32),
            pltpu.VMEM((81, 128), F32),
            pltpu.VMEM((81, 128), F32),
            pltpu.VMEM(TILE, F32),
            pltpu.VMEM((3,) + TILE, F32),
            pltpu.VMEM((27, 2, 128), F32),
        ],
        scratch_shapes=[
            pltpu.VMEM((2, 5, 4, 4) + TILE, F32),
            pltpu.VMEM(TILE, jnp.int32),
            pltpu.SemaphoreType.DMA((7,)),
        ],
        name="traces",
    )(lam, cube, blk, coords, disp)


def first_face_call(grad, u, own, received, gkeep, cols, g):
    return pl.pallas_call(
        first_face_kernel,
        in_specs=[HBM] + [VMEM] * 6,
        out_specs=[HBM, VMEM, VMEM],
        out_shape=[
            jax.ShapeDtypeStruct((5, 64) + TILE, F32),
            pltpu.VMEM((2, 3) + TILE, F32),
            pltpu.VMEM((6, 128), F32),
        ],
        scratch_shapes=[pltpu.VMEM((5, 16) + TILE, F32), pltpu.SemaphoreType.DMA((4,))],
        input_output_aliases={0: 0},
        name="faces_first",
    )(grad, *near(u, own, received, gkeep, cols, g))


def label_call(even, odd, far, rows, nb):
    return pl.pallas_call(
        functools.partial(label_kernel, nb),
        in_specs=[VMEM] * 4,
        out_specs=VMEM,
        out_shape=pltpu.VMEM((32, 128), F32),
        name="labels",
    )(*near(even, odd, far, rows))


def second_face_call(grad, u, own, received, gkeep, cols, g, part, rows, mine, labels, cpack, nb, cap, px):
    height = -(-15 * cap // 128)
    return pl.pallas_call(
        functools.partial(second_face_kernel, nb, cap, px),
        in_specs=[HBM] + [VMEM] * 11,
        out_specs=[HBM, VMEM, VMEM, VMEM],
        out_shape=[
            jax.ShapeDtypeStruct((5, 64) + TILE, F32),
            pltpu.VMEM((nb * height, 128), F32),
            pltpu.VMEM((2, 3) + TILE, F32),
            pltpu.VMEM((6, 128), F32),
        ],
        scratch_shapes=[
            pltpu.VMEM((5, 16) + TILE, F32),
            pltpu.VMEM((6 * nb, 1024), jnp.bfloat16),
            pltpu.VMEM((128, 1024), jnp.bfloat16),
            pltpu.SemaphoreType.DMA((4,)),
        ],
        input_output_aliases={0: 0},
        name="faces_second",
    )(grad, *near(u, own, received, gkeep, cols, g, part, rows, mine, labels, cpack))


def slot_call(blk, coords, nb, cap):
    return pl.pallas_call(
        functools.partial(slot_kernel, nb, cap),
        in_specs=[VMEM, VMEM],
        out_specs=[VMEM, VMEM],
        out_shape=[
            pltpu.VMEM((16, 128), F32),
            pltpu.VMEM((3 * nb, 128), F32),
        ],
        scratch_shapes=[
            pltpu.VMEM((9 * nb, 1024), jnp.bfloat16),
            pltpu.VMEM((128, 1024), jnp.bfloat16),
        ],
        name="slots",
    )(*near(blk, coords))


def lattice_call(buf, part, yrow, xrow, nb, cap, py):
    return pl.pallas_call(
        functools.partial(lattice_kernel, nb, cap, py),
        in_specs=[VMEM] * 4,
        out_shape=[
            jax.ShapeDtypeStruct((3,) + TILE, F32),
            jax.ShapeDtypeStruct((3, 1, LU * LV * LW), F32),
        ],
        scratch_shapes=[
            pltpu.VMEM((16 * 3 * LU, 128), F32),
            pltpu.VMEM((16 * LV * LW, 128), F32),
        ],
        name="lattice",
    )(*near(buf, part, yrow, xrow))


def shift_px(payload, step):
    length = lax.axis_size("px")
    pairs = [(i, i + step) for i in range(length) if 0 <= i + step < length]
    return lax.ppermute(payload, "px", pairs)


def shift_py(payload, step):
    length = lax.axis_size("py")
    return lax.ppermute(payload, "py", [(i, (i + step) % length) for i in range(length)])


def swap(payload, axis, start, wrap):
    length = lax.axis_size(axis)
    pairs = []
    for i in range(start, length, 2):
        j = (i + 1) % length
        if i + 1 < length or wrap:
            pairs += [(i, j), (j, i)]
    return lax.ppermute(payload, axis, pairs)


def per_device(flow_state, adjoint, displacement, lattice_block, lattice_coords):
    px = lax.axis_size("px")
    py = lax.axis_size("py")
    assert px % 2 == 0 and py % 2 == 0
    nb = px * py
    cap = 2 * 1024 // nb
    u = flow_state.reshape(5, 64, 8, 128)
    lam = adjoint.reshape(5, 64, 8, 128)
    own_even, own_odd, y_even, y_odd, blk, coords, disp = trace_call(
        lam,
        adjoint.reshape(5, 4, 4, 4, 8, 128),
        lattice_block.reshape(8, 128),
        lattice_coords.reshape(3, 8, 128),
        displacement.transpose(0, 2, 1, 3).reshape(27, 2, 128),
    )
    first = swap(own_even, "px", 0, False)
    second = swap(own_odd, "px", 1, False)
    even = swap(y_even, "py", 0, True)
    odd = swap(y_odd, "py", 1, True)
    mine, cpack = slot_call(blk, coords, nb, cap)
    beside = jnp.where(lax.axis_index("py") % 2 == 0, even[80:81], odd[80:81])
    far = shift_px(jnp.concatenate([blk, beside]), -1)
    grad, ukeep, gkeep, cols, g = volume_call(u, lam, disp, even, odd)
    grad, part, rows = first_face_call(grad, ukeep, own_even, first, gkeep, cols, g)
    labels = label_call(even, odd, far, rows, nb)
    grad, buf, part, rows = second_face_call(
        grad, ukeep, own_odd, second, gkeep, cols, g, part, rows, mine, labels, cpack, nb, cap, px
    )
    received = lax.all_to_all(buf, ("px", "py"), split_axis=0, concat_axis=0, tiled=True)
    yrow = shift_py(rows, 1)
    below = jnp.pad(yrow[3:6, None, :], ((0, 0), (0, 7), (0, 0)))
    xrow = shift_px(part[1] + below, 1)
    owned, lattice = lattice_call(received, part, yrow, xrow, nb, cap, py)
    return (
        grad.reshape(5, 64, 1, 8, 128),
        owned.reshape(3, 1, 8, 128),
        lattice.reshape(1, 1, 3, LU * LV * LW),
    )


def solution(mesh):
    in_specs = (
        P(None, None, "px", "py", None),
        P(None, None, "px", "py", None),
        P(None, "px", "py", None),
        P("px", "py", None, None),
        P("px", "py", None, None),
    )
    out_specs = (
        P(None, None, "px", "py", None),
        P(None, "px", "py", None),
        P("px", "py", None, None),
    )
    return jax.shard_map(
        per_device, mesh=mesh, in_specs=in_specs, out_specs=out_specs, check_vma=False
    )
```

time: 51.9 us -> 40 us (0.77)
  local copies, waits for them, and re-layouts: 9.03 us -> 0.02 us
  waiting for transfers between devices: 4.64 us -> 10.1 us
  starting transfers between devices: 21.1 us -> 16.2 us
  Pallas kernels: 15.4 us -> 12.4 us
    ppermute x4 -> x2, starting transfers between devices: 11.8 us -> 4.96 us  [shift_px(): return lax.ppermute(payload, 'px', pairs)]
    ppermute x0 -> x4, starting transfers between devices: none -> 6.03 us  [swap(): return lax.ppermute(payload, axis, pairs)]
    ppermute x0 -> x4, waiting for transfers between devices: none -> 5.9 us  [swap(): return lax.ppermute(payload, axis, pairs)]
    unnamed x27 -> x4, local copies, waits for them, and re-layouts: 5.24 us -> 0.01 us
    all_to_all x1, starting transfers between devices: 8.09 us -> 4.92 us  [per_device(): lax.all_to_all(buf, ('px', 'py'), split_axis=0, concat_axis=0, tiled=True)]
    pallas_call x4 -> x7, Pallas kernels: 15.4 us -> 12.4 us  [the longest x1 5.19 us: volume_call(): pl.pallas_call(volume_kernel, in_specs=[HBM, HBM, VMEM, VMEM, VMEM], out_...]
    slice x4 -> x1, local copies, waits for them, and re-layouts: 2.29 us -> 0.01 us  [per_device(): below = jnp.pad(yrow[3:6, None, :], ((0, 0), (0, 7), (0, 0)))]
    ppermute x3 -> x1, starting transfers between devices: 1.22 us -> 0.3 us  [shift_py(): lax.ppermute(payload, 'py', [(i, (i + step) % length) for i in range(leng...]
  transfers between devices with their start and end apart: 8 -> 8, of which waited for: 3 -> 4; matrix products, arithmetic and copies ran while one was open for 8% -> 0% of each run, Pallas kernels for 17% -> 18%
where the time goes in v2:
time: 40 us; the launch traced here: 39.6 us
  starting transfers between devices  16.2 us (40%)
  Pallas kernels  12.4 us (31%)
  waiting for transfers between devices  10.1 us (25%)
  between operations  0.76 us (2%)
    ppermute x4, starting transfers between devices, swap(): return lax.ppermute(payload, axis, pairs)  6.03 us
    ppermute x4, waiting for transfers between devices, swap(): return lax.ppermute(payload, axis, pairs)  5.9 us
    pallas_call x1, Pallas kernels, volume_call(): pl.pallas_call(volume_kernel, in_specs=[HBM, HBM, VMEM, VMEM, VMEM], out_...  5.19 us
    ppermute x2, starting transfers between devices, shift_px(): return lax.ppermute(payload, 'px', pairs)  4.96 us
    all_to_all x1, starting transfers between devices, per_device(): lax.all_to_all(buf, ('px', 'py'), split_axis=0, concat_axis=0, tiled=True)  4.92 us
    ppermute x1, waiting for transfers between devices, shift_py(): lax.ppermute(payload, 'py', [(i, (i + step) % length) for i in range(leng...  2.78 us
    pallas_call x1, Pallas kernels, second_face_call(): pl.pallas_call(functools.partial(second_face_kernel, nb, cap, px), in_spe...  2.61 us
    pallas_call x1, Pallas kernels, lattice_call(): pl.pallas_call(functools.partial(lattice_kernel, nb, cap, py), in_specs=[...  1.45 us
  transfers between devices with their start and end apart: 8, of which 4 were waited for; matrix products, arithmetic and copies ran while one was open for 0% of the time, Pallas kernels for 18%

profile of v2, /device:TPU:0, one launch (start us, length us, event | category | flops | bytes accessed | tf_op | source)
XLA Modules:
  0.0 39.6 jit_solution(357580403601859678)
XLA Ops:
  0.6 1.4 %traces.1 = (f32[5,16,8,128]{3,2,1,0:T(8,128)S(1)}, f32[5,16,8,128]{3,2,1,0:T(8,128)S(1)}, f32[81,128]{1,0:T(8,128)S(1)}, f32[81,128]{1,0:T(8,128)S(1)}, f32[8,1...) custom-call(f32[5,64,8,128]{3,2,1,0:T(8,128)} %bitcast.22, f32[5,4,4,4,8,128]{5,4,3,2,1,0:T(8,128)} %bitcast.23, ...), custom_call_target="tpu_custom_call" | custom-call | tf_op jit(solution)/shard_map/traces/pallas_call | solution.py:618
  2.0 0.0 copy-start
  2.0 0.5 %collective-permute-start = (f32[81,128]{1,0:T(8,128)S(1)}, f32[81,128]{1,0:T(8,128)S(1)}, u32[]{:S(2)}, u32[]{:S(2)}) collective-permute-start(f32[81,128]{1,0:T(8,128)S(1)} %get-tuple-element.27), channel_id=1, source_target_pairs={{0,1},{1,0},{2,3},{3,2},{4,5},{5,4},{6,7},{7,6},{8,9},{9,8},{10,11... | collective-permute-start | bytes 124424 | tf_op jit(solution)/shard_map/ppermute | solution.py:740
  2.5 2.6 %collective-permute-start.1 = (f32[81,128]{1,0:T(8,128)S(1)}, f32[81,128]{1,0:T(8,128)S(1)}, u32[]{:S(2)}, u32[]{:S(2)}) collective-permute-start(f32[81,128]{1,0:T(8,128)S(1)} %get-tuple-element.28), channel_id=1, source_target_pairs={{1,2},{2,1},{3,0},{0,3},{5,6},{6,5},{7,4},{4,7},{9,10},{10,9},{11,... | collective-permute-start | bytes 124424 | tf_op jit(solution)/shard_map/ppermute | solution.py:740
  5.2 1.5 %collective-permute-start.2 = (f32[5,16,8,128]{3,2,1,0:T(8,128)S(1)}, f32[5,16,8,128]{3,2,1,0:T(8,128)S(1)}, u32[]{:S(2)}, u32[]{:S(2)}) collective-permute-start(f32[5,16,8,128]{3,2,1,0:T(8,128)S(1)} %get-tuple-element.31.own_ref), channel_id=1, source_target_pairs={{0,4},{4,0},{8,12},{12,8},{16,20},{20,16},{24,28},{28,24},{1,5},{5... | collective-permute-start | bytes 983048 | tf_op jit(solution)/shard_map/ppermute | solution.py:740
  6.7 1.4 %collective-permute-start.3 = (f32[5,16,8,128]{3,2,1,0:T(8,128)S(1)}, f32[5,16,8,128]{3,2,1,0:T(8,128)}, u32[]{:S(2)}, u32[]{:S(2)}) collective-permute-start(f32[5,16,8,128]{3,2,1,0:T(8,128)S(1)} %get-tuple-element.36.own_ref), channel_id=1, source_target_pairs={{4,8},{8,4},{12,16},{16,12},{20,24},{24,20},{5,9},{9,5},{13,17},{1... | collective-permute-start | bytes 983048 | tf_op jit(solution)/shard_map/ppermute | solution.py:740
  8.1 0.0 collective-permute-done.even_ref
  8.1 0.0 collective-permute-done.1.odd_ref
  8.1 1.3 %collective-permute-start.4 = (f32[9,128]{1,0:T(8,128)S(1)}, f32[9,128]{1,0:T(8,128)S(1)}, u32[]{:S(2)}, u32[]{:S(2)}) collective-permute-start(f32[9,128]{1,0:T(8,128)S(1)} %pad_maximum_fusion), channel_id=1, source_target_pairs={{4,0},{8,4},{12,8},{16,12},{20,16},{24,20},{28,24},{5,1},{9,5},{13... | collective-permute-start | bytes 13832 | tf_op jit(solution)/shard_map/ppermute | solution.py:725
  9.4 0.6 %slots.1 = (f32[16,128]{1,0:T(8,128)S(1)}, f32[96,128]{1,0:T(8,128)S(1)}) custom-call(f32[8,128]{1,0:T(8,128)S(1)} %get-tuple-element.39.blk_ref, f32[3,8,128]{2,1,0:T(8,128)S(1)} %get-tuple-element.40.coords_ref), custom_call_target="tpu_custom_call" | custom-call | tf_op jit(solution)/shard_map/slots/pallas_call | solution.py:690
  10.0 5.2 %volume.1 = (f32[5,64,8,128]{3,2,1,0:T(8,128)}, f32[2,5,16,8,128]{4,3,2,1,0:T(8,128)S(1)}, f32[2,5,16,8,128]{4,3,2,1,0:T(8,128)S(1)}, f32[2,2,4,3,8,128]{5,4,3,2,1,0:T(8,128)S(1)}, f32[2,3,2,8,128]{4,3,2,1,0:T(8,128)S(1)}) custom-call(f32[5,64,8,128]{3,2,1,0:T(8,128)} %bitcast.26, f32[5,64,8,128]{3,2,1,0:T(8,128)} %bitcast.24, ...), custom_call_target="tpu_custom_call" | custom-call | tf_op jit(solution)/shard_map/volume/pallas_call | solution.py:590
  15.2 5.9 %collective-permute-done.2.received_ref = f32[5,16,8,128]{3,2,1,0:T(8,128)S(1)} collective-permute-done((f32[5,16,8,128]{3,2,1,0:T(8,128)S(1)}, f32[5,16,8,128]{3,2,1,0:T(8,128)S(1)}, u32[]{:S(2)}, u32[]{:S(2)}) %collective-permute-start.2) | collective-permute-done | bytes 327712 | tf_op jit(solution)/shard_map/ppermute | solution.py:740
  21.1 1.0 %faces_first.1 = (f32[5,64,8,128]{3,2,1,0:T(8,128)}, f32[2,3,8,128]{3,2,1,0:T(8,128)S(1)}, f32[6,128]{1,0:T(8,128)S(1)}) custom-call(f32[5,64,8,128]{3,2,1,0:T(8,128)} %get-tuple-element.29.grad_in_ref, f32[2,5,16,8,128]{4,3,2,1,0:T(8,128)S(1)} %get-tuple-element.30.u_ref, ...), custom_call_target="tpu_custom_call", output_to_operand_aliasing={{0}: (0, {})} | custom-call | tf_op jit(solution)/shard_map/faces_first/pallas_call | solution.py:641
  22.1 0.0 collective-permute-done.4.far_ref
  22.1 0.2 labels.1.label_ref
  22.3 0.0 collective-permute-done.3.received_ref
  22.3 2.6 %faces_second.1 = (f32[5,64,8,128]{3,2,1,0:T(8,128)}, f32[256,128]{1,0:T(8,128)}, f32[2,3,8,128]{3,2,1,0:T(8,128)S(1)}, f32[6,128]{1,0:T(8,128)S(1)}) custom-call(f32[5,64,8,128]{3,2,1,0:T(8,128)} %get-tuple-element.35.grad_in_ref, f32[2,5,16,8,128]{4,3,2,1,0:T(8,128)S(1)} %get-tuple-element.30.u_ref, ...), custom_call_target="tpu_custom_call", output_to_operand_aliasing={{0}: (0, {})} | custom-call | tf_op jit(solution)/shard_map/faces_second/pallas_call | solution.py:668
  25.0 4.9 %all-to-all-start = ((f32[32,8,128]{2,1,0:T(8,128)}), f32[32,8,128]{2,1,0:T(8,128)S(1)}, u32[]{:S(2)}, u32[]{:S(2)}) async-start(f32[32,8,128]{2,1,0:T(8,128)} %bitcast.9), calls=%async_computation | async-start | bytes 262144 | tf_op jit(solution)/shard_map/all_to_all | solution.py:771
  29.9 0.3 collective-permute-start.5
  30.2 2.8 %collective-permute-done.5.yrow_ref = f32[6,128]{1,0:T(8,128)S(1)} collective-permute-done((f32[6,128]{1,0:T(8,128)S(1)}, f32[6,128]{1,0:T(8,128)S(1)}, u32[]{:S(2)}, u32[]{:S(2)}) %collective-permute-start.5) | collective-permute-done | bytes 3104 | tf_op jit(solution)/shard_map/ppermute | solution.py:730
  33.0 3.7 %collective-permute-start.6 = (f32[3,8,128]{2,1,0:T(8,128)S(1)}, f32[3,8,128]{2,1,0:T(8,128)S(1)}, u32[]{:S(2)}, u32[]{:S(2)}) collective-permute-start(f32[3,8,128]{2,1,0:T(8,128)S(1)} %bitcast_add_fusion), channel_id=1, source_target_pairs={{0,4},{4,8},{8,12},{12,16},{16,20},{20,24},{24,28},{1,5},{5,9},{9,... | collective-permute-start | bytes 36872 | tf_op jit(solution)/shard_map/ppermute | solution.py:725
  36.7 1.4 %collective-permute-done.6.xrow_ref = f32[3,8,128]{2,1,0:T(8,128)S(1)} collective-permute-done((f32[3,8,128]{2,1,0:T(8,128)S(1)}, f32[3,8,128]{2,1,0:T(8,128)S(1)}, u32[]{:S(2)}, u32[]{:S(2)}) %collective-permute-start.6) | collective-permute-done | bytes 12320 | tf_op jit(solution)/shard_map/ppermute | solution.py:725
  38.1 0.1 all-to-all-done
  38.1 1.5 %lattice.1 = (f32[3,8,128]{2,1,0:T(8,128)}, f32[3,1,864]{2,1,0:T(1,128)}) custom-call(f32[256,128]{1,0:T(8,128)S(1)} %bitcast.21, f32[2,3,8,128]{3,2,1,0:T(8,128)S(1)} %get-tuple-element.45.part_ref, f32[6,128]{1,0:T(8,128)S(1)} %collective-permute-done.5.yrow_ref, f32[3,8,128]{2,1,0:T(8,128)S(1)} %collective-permute-done.6.xrow_ref), custom_call_target="tpu_custom_call" | custom-call | tf_op jit(solution)/shard_map/lattice/pallas_call | solution.py:707
  (8 shorter events, 0.0 us)
Async XLA Ops:
  2.0 13.2 %copy-start = (f32[5,16,8,128]{3,2,1,0:T(8,128)}, f32[5,16,8,128]{3,2,1,0:T(8,128)S(1)}, u32[]{:S(2)}) copy-start(f32[5,16,8,128]{3,2,1,0:T(8,128)S(1)} %get-tuple-element.36.own_ref) | copy-start | bytes 983044
  2.0 6.0 %collective-permute-start = (f32[81,128]{1,0:T(8,128)S(1)}, f32[81,128]{1,0:T(8,128)S(1)}, u32[]{:S(2)}, u32[]{:S(2)}) collective-permute-start(f32[81,128]{1,0:T(8,128)S(1)} %get-tuple-element.27), channel_id=1, source_target_pairs={{0,1},{1,0},{2,3},{3,2},{4,5},{5,4},{6,7},{7,6},{8,9},{9,8},{10,11... | collective-permute-start | bytes 124424 | tf_op jit(solution)/shard_map/ppermute | solution.py:740
  2.5 5.5 %collective-permute-start.1 = (f32[81,128]{1,0:T(8,128)S(1)}, f32[81,128]{1,0:T(8,128)S(1)}, u32[]{:S(2)}, u32[]{:S(2)}) collective-permute-start(f32[81,128]{1,0:T(8,128)S(1)} %get-tuple-element.28), channel_id=1, source_target_pairs={{1,2},{2,1},{3,0},{0,3},{5,6},{6,5},{7,4},{4,7},{9,10},{10,9},{11,... | collective-permute-start | bytes 124424 | tf_op jit(solution)/shard_map/ppermute | solution.py:740
  5.2 15.9 %collective-permute-start.2 = (f32[5,16,8,128]{3,2,1,0:T(8,128)S(1)}, f32[5,16,8,128]{3,2,1,0:T(8,128)S(1)}, u32[]{:S(2)}, u32[]{:S(2)}) collective-permute-start(f32[5,16,8,128]{3,2,1,0:T(8,128)S(1)} %get-tuple-element.31.own_ref), channel_id=1, source_target_pairs={{0,4},{4,0},{8,12},{12,8},{16,20},{20,16},{24,28},{28,24},{1,5},{5... | collective-permute-start | bytes 983048 | tf_op jit(solution)/shard_map/ppermute | solution.py:740
  6.7 15.6 %collective-permute-start.3 = (f32[5,16,8,128]{3,2,1,0:T(8,128)S(1)}, f32[5,16,8,128]{3,2,1,0:T(8,128)}, u32[]{:S(2)}, u32[]{:S(2)}) collective-permute-start(f32[5,16,8,128]{3,2,1,0:T(8,128)S(1)} %get-tuple-element.36.own_ref), channel_id=1, source_target_pairs={{4,8},{8,4},{12,16},{16,12},{20,24},{24,20},{5,9},{9,5},{13,17},{1... | collective-permute-start | bytes 983048 | tf_op jit(solution)/shard_map/ppermute | solution.py:740
  8.1 14.0 %collective-permute-start.4 = (f32[9,128]{1,0:T(8,128)S(1)}, f32[9,128]{1,0:T(8,128)S(1)}, u32[]{:S(2)}, u32[]{:S(2)}) collective-permute-start(f32[9,128]{1,0:T(8,128)S(1)} %pad_maximum_fusion), channel_id=1, source_target_pairs={{4,0},{8,4},{12,8},{16,12},{20,16},{24,20},{28,24},{5,1},{9,5},{13... | collective-permute-start | bytes 13832 | tf_op jit(solution)/shard_map/ppermute | solution.py:725
  21.1 1.3 %copy-start.1 = (f32[5,16,8,128]{3,2,1,0:T(8,128)S(1)}, f32[5,16,8,128]{3,2,1,0:T(8,128)}, u32[]{:S(2)}) copy-start(f32[5,16,8,128]{3,2,1,0:T(8,128)} %copy-done) | copy-start | bytes 983044
  25.0 13.2 %all-to-all-start = ((f32[32,8,128]{2,1,0:T(8,128)}), f32[32,8,128]{2,1,0:T(8,128)S(1)}, u32[]{:S(2)}, u32[]{:S(2)}) async-start(f32[32,8,128]{2,1,0:T(8,128)} %bitcast.9), calls=%async_computation | async-start | bytes 262144 | tf_op jit(solution)/shard_map/all_to_all | solution.py:771
  29.9 3.1 %collective-permute-start.5 = (f32[6,128]{1,0:T(8,128)S(1)}, f32[6,128]{1,0:T(8,128)S(1)}, u32[]{:S(2)}, u32[]{:S(2)}) collective-permute-start(f32[6,128]{1,0:T(8,128)S(1)} %get-tuple-element.46), channel_id=1, source_target_pairs={{0,1},{1,2},{2,3},{3,0},{4,5},{5,6},{6,7},{7,4},{8,9},{9,10},{10,1... | collective-permute-start | bytes 9224 | tf_op jit(solution)/shard_map/ppermute | solution.py:730
  33.0 5.1 %collective-permute-start.6 = (f32[3,8,128]{2,1,0:T(8,128)S(1)}, f32[3,8,128]{2,1,0:T(8,128)S(1)}, u32[]{:S(2)}, u32[]{:S(2)}) collective-permute-start(f32[3,8,128]{2,1,0:T(8,128)S(1)} %bitcast_add_fusion), channel_id=1, source_target_pairs={{0,4},{4,8},{8,12},{12,16},{16,20},{20,24},{24,28},{1,5},{5,9},{9,... | collective-permute-start | bytes 36872 | tf_op jit(solution)/shard_map/ppermute | solution.py:725

commit v3 on v2

--- a/solution.py
+++ b/solution.py
@@ -157,8 +157,8 @@
     copies = [
         pltpu.make_async_copy(lam_ref.at[:, pl.ds(48 - 48 * x_odd, 16)], own_even, sem.at[0]),
         pltpu.make_async_copy(lam_ref.at[:, pl.ds(48 * x_odd, 16)], own_odd, sem.at[1]),
-        pltpu.make_async_copy(cube_ref.at[:, :, 0], tiles.at[0], sem.at[2]),
-        pltpu.make_async_copy(cube_ref.at[:, :, 3], tiles.at[1], sem.at[3]),
+        pltpu.make_async_copy(cube_ref.at[:, :, 0, :, pl.ds(0, 1)], tiles.at[0, :, :, :, pl.ds(0, 1)], sem.at[2]),
+        pltpu.make_async_copy(cube_ref.at[:, :, 3, :, pl.ds(7, 1)], tiles.at[1, :, :, :, pl.ds(7, 1)], sem.at[3]),
         pltpu.make_async_copy(blk_ref, blocks, sem.at[4]),
         pltpu.make_async_copy(coords_ref, coords, sem.at[5]),
         pltpu.make_async_copy(disp_ref, disp, sem.at[6]),
@@ -180,13 +180,40 @@
         copy.wait()
 
 
-def volume_kernel(u_ref, lam_ref, disp_ref, even_ref, odd_ref, grad_ref, ukeep, gkeep, cols, g_ref, lam, umid, gmid, j0t, j1t, j2t, j0b, j1b, j2b, s1, s2, yj, sem):
+def own_slots(nb, cap, blk_ref, coords_ref, mine_ref, cpack_ref, lhs, rhs):
+    mine_ref[0:8, :] = blk_ref[...]
+    slot_of = (lax.broadcasted_iota(jnp.int32, (128, 128), 0) & (cap - 1)).astype(F32)
+
+    def emit(y, here, rank):
+        mine_ref[8 + y : 9 + y, :] = rank
+        lanes = pl.ds(128 * y, 128)
+        rhs[:, lanes] = jnp.where(jnp.broadcast_to(rank, (128, 128)) == slot_of, 1.0, 0.0).astype(jnp.bfloat16)
+        for k in range(3):
+            rest = coords_ref[k, y : y + 1, :]
+            for part in range(3):
+                piece = rest.astype(jnp.bfloat16).astype(F32)
+                rest = rest - piece
+                lhs[pl.ds((3 * part + k) * nb, nb), lanes] = (
+                    here * jnp.broadcast_to(piece, (nb, 128))
+                ).astype(jnp.bfloat16)
+
+    block_ranks(nb, [[blk_ref[y : y + 1, :] for y in range(8)]], emit)
+    total = lax.dot_general(lhs[...], rhs[...], (((1,), (1,)), ((), ())), preferred_element_type=F32)
+    cpack_ref[...] = total[0 : 3 * nb] + total[3 * nb : 6 * nb] + total[6 * nb : 9 * nb]
+
+
+def volume_kernel(nb, cap, u_ref, lam_ref, disp_ref, even_ref, odd_ref, blk_ref, coords_ref, grad_ref, lkeep, ukeep, gkeep, cols, g_ref, mine_ref, cpack_ref, lam, umid, gmid, j0t, j1t, j2t, j0b, j1b, j2b, s1, s2, yj, lhs, rhs, sem):
     lam_copies = [pltpu.make_async_copy(lam_ref.at[f], lam.at[f], sem.at[f]) for f in range(5)]
     u_at = [ukeep.at[0], umid.at[0], umid.at[1], ukeep.at[1]]
     g_at = [gkeep.at[0], gmid.at[0], gmid.at[1], gkeep.at[1]]
     u_copies = [pltpu.make_async_copy(u_ref.at[:, pl.ds(16 * a, 16)], u_at[a], sem.at[5 + a]) for a in range(4)]
-    for copy in lam_copies + u_copies:
+    keep_copies = [
+        pltpu.make_async_copy(lam_ref.at[:, pl.ds(48 * side, 16)], lkeep.at[side], sem.at[11 + side])
+        for side in range(2)
+    ]
+    for copy in lam_copies + u_copies + keep_copies:
         copy.start()
+    own_slots(nb, cap, blk_ref, coords_ref, mine_ref, cpack_ref, lhs, rhs)
 
     for c in range(3):
         x = [[with_next(corner(disp_ref, c, e1, e2)) for e2 in range(2)] for e1 in range(2)]
@@ -307,7 +334,7 @@
         for e1 in range(2):
             for e2 in range(2):
                 g_ref[e1, c, e2] = gx[e1][e2][0] + pltpu.roll(gx[e1][e2][1], 1, 1)
-    for copy in mid_copies:
+    for copy in mid_copies + keep_copies:
         copy.wait()
 
 
@@ -321,7 +348,7 @@
             n = 4 * b + c
             weight = float(WEIGHTS[b] * WEIGHTS[c])
             u = [u_ref[side, f, n] for f in range(5)]
-            own = [own_ref[f, n] for f in range(5)]
+            own = [own_ref[side, f, n] for f in range(5)]
             normal = cross(col1[c], col2)
             if wall:
                 inverse, v, v2, p, ep = primitives(u)
@@ -350,11 +377,11 @@
                 back = node.face(normal, vn, jump, sigma)
                 grads = node.gradient()
             for f in range(5):
-                gout[f, n] = gkeep[side, f, n] + grads[f]
+                gout[side, f, n] = gkeep[side, f, n] + grads[f]
             back1[c] = add3(back1[c], cross(col2, back))
             back2[b] = add3(back2[b], cross(back, col1[c]))
         pltpu.make_async_copy(
-            gout.at[:, pl.ds(4 * b, 4)], grad_ref.at[:, pl.ds(48 * side + 4 * b, 4)], sem.at[b]
+            gout.at[side, :, pl.ds(4 * b, 4)], grad_ref.at[:, pl.ds(48 * side + 4 * b, 4)], sem.at[side, b]
         ).start()
     rows = lax.broadcasted_iota(jnp.int32, TILE, 0)
     for k in range(3):
@@ -370,7 +397,7 @@
 def wait_side(side, grad_ref, gout, sem):
     for b in range(4):
         pltpu.make_async_copy(
-            gout.at[:, pl.ds(4 * b, 4)], grad_ref.at[:, pl.ds(48 * side + 4 * b, 4)], sem.at[b]
+            gout.at[side, :, pl.ds(4 * b, 4)], grad_ref.at[:, pl.ds(48 * side + 4 * b, 4)], sem.at[side, b]
         ).wait()
 
 
@@ -394,14 +421,7 @@
             i += 1
 
 
-def first_face_kernel(grad_in_ref, u_ref, own_ref, received_ref, gkeep, cols, g_ref, grad_ref, part_ref, row_ref, gout, sem):
-    side = 1 - lax.axis_index("px") % 2
-    sign = jnp.where(side == 0, F32(-1.0), F32(1.0))
-    one_side(side, 0.5 * sign, sign, False, u_ref, own_ref, received_ref, gkeep, cols, g_ref, grad_ref, part_ref, row_ref, gout, sem)
-    wait_side(side, grad_ref, gout, sem)
-
-
-def label_kernel(nb, even_ref, odd_ref, far_ref, row_ref, label_ref):
+def far_labels(nb, even_ref, odd_ref, far_ref, label_ref):
     beside = jnp.where(lax.axis_index("py") % 2 == 0, even_ref[80:81, :], odd_ref[80:81, :])
     across = far_ref[8:9, :]
     label_ref[0:8, :] = far_ref[0:8, :]
@@ -414,24 +434,29 @@
     block_ranks(nb, [[far_ref[y : y + 1, :] for y in range(8)], [beside], [across]], emit)
 
 
-def second_face_kernel(nb, cap, px, grad_in_ref, u_ref, own_ref, received_ref, gkeep, cols, g_ref, part_in_ref, row_in_ref, mine_ref, label_ref, cpack_ref, grad_ref, buf_ref, part_ref, row_ref, gout, lhs, rhs, sem):
+def face_kernel(nb, cap, px, even_recv, odd_recv, grad_in_ref, own_ref, u_ref, gkeep, cols, g_ref, mine_ref, even_ref, odd_ref, far_ref, cpack_ref, grad_ref, buf_ref, part_ref, row_ref, gout, label_ref, lhs, rhs, sem):
     index = lax.axis_index("px")
     side = index % 2
     is_first = index == 0
     is_last = index == px - 1
-    part_ref[1 - side] = part_in_ref[1 - side]
-    row_ref[...] = row_in_ref[...]
-    rest = (u_ref, own_ref, received_ref, gkeep, cols, g_ref, grad_ref, part_ref, row_ref, gout, sem)
+
+    def run(at, scale, sigma, wall, received_ref):
+        one_side(at, scale, sigma, wall, u_ref, own_ref, received_ref, gkeep, cols, g_ref, grad_ref, part_ref, row_ref, gout, sem)
+
+    sign = jnp.where(side == 1, F32(-1.0), F32(1.0))
+    run(1 - side, 0.5 * sign, sign, False, even_recv)
 
     @pl.when(is_first)
     def _():
-        one_side(side, None, None, True, *rest)
+        run(side, None, None, True, None)
 
     @pl.when(jnp.logical_not(is_first))
     def _():
         scale = jnp.where(side == 0, F32(-0.5), jnp.where(is_last, F32(1.0), F32(0.5)))
         sigma = jnp.where(side == 0, F32(-1.0), jnp.where(is_last, F32(0.0), F32(1.0)))
-        one_side(side, scale, sigma, False, *rest)
+        run(side, scale, sigma, False, odd_recv)
+
+    far_labels(nb, even_ref, odd_ref, far_ref, label_ref)
 
     block_of = lax.broadcasted_iota(jnp.int32, (nb, 128), 0).astype(F32)
     slot_of = (lax.broadcasted_iota(jnp.int32, (128, 128), 0) & (cap - 1)).astype(F32)
@@ -473,29 +498,8 @@
         for i, item in enumerate(inside[1:], 1):
             value = jnp.where(position == i, item, value)
         buf_ref[pl.ds(r, nb, stride=height), :] = value
-    wait_side(side, grad_ref, gout, sem)
-
-
-def slot_kernel(nb, cap, blk_ref, coords_ref, mine_ref, cpack_ref, lhs, rhs):
-    mine_ref[0:8, :] = blk_ref[...]
-    slot_of = (lax.broadcasted_iota(jnp.int32, (128, 128), 0) & (cap - 1)).astype(F32)
-
-    def emit(y, here, rank):
-        mine_ref[8 + y : 9 + y, :] = rank
-        lanes = pl.ds(128 * y, 128)
-        rhs[:, lanes] = jnp.where(jnp.broadcast_to(rank, (128, 128)) == slot_of, 1.0, 0.0).astype(jnp.bfloat16)
-        for k in range(3):
-            rest = coords_ref[k, y : y + 1, :]
-            for part in range(3):
-                piece = rest.astype(jnp.bfloat16).astype(F32)
-                rest = rest - piece
-                lhs[pl.ds((3 * part + k) * nb, nb), lanes] = (
-                    here * jnp.broadcast_to(piece, (nb, 128))
-                ).astype(jnp.bfloat16)
-
-    block_ranks(nb, [[blk_ref[y : y + 1, :] for y in range(8)]], emit)
-    total = lax.dot_general(lhs[...], rhs[...], (((1,), (1,)), ((), ())), preferred_element_type=F32)
-    cpack_ref[...] = total[0 : 3 * nb] + total[3 * nb : 6 * nb] + total[6 * nb : 9 * nb]
+    for at in range(2):
+        wait_side(at, grad_ref, gout, sem)
 
 
 def powers(t, degree):
@@ -561,17 +565,20 @@
     for b in range(LV):
         for c in range(LW):
             rhs[pl.ds(16 * (LW * b + c), 16), :] = bv[b] * bw[c]
-    left = jnp.concatenate([lhs[pl.ds(i, 3 * LU, stride=16), :] for i in range(16)], axis=1)
+    lhs[pl.ds(16 * 3 * LU, 64), :] = jnp.zeros((64, 128), F32)
+    rows = 3 * LU + 4
+    left = jnp.concatenate([lhs[pl.ds(i, rows, stride=16), :] for i in range(16)], axis=1)
     right = jnp.concatenate([rhs[pl.ds(i, LV * LW, stride=16), :] for i in range(16)], axis=1)
-    left_high = left.astype(jnp.bfloat16)
-    left_low = (left - left_high.astype(F32)).astype(jnp.bfloat16)
-    right_high = right.astype(jnp.bfloat16)
-    right_low = (right - right_high.astype(F32)).astype(jnp.bfloat16)
-
-    def product(x, y):
-        return lax.dot_general(x, y, (((1,), (1,)), ((), ())), preferred_element_type=F32)
-
-    total = product(left_high, right_high) + (product(left_high, right_low) + product(left_low, right_high))
+
+    def two_pieces(value):
+        high = value.astype(jnp.bfloat16).astype(F32)
+        return jnp.concatenate([high, value - high], axis=0).astype(jnp.bfloat16)
+
+    both = lax.dot_general(
+        two_pieces(left), two_pieces(right), (((1,), (1,)), ((), ())), preferred_element_type=F32
+    )
+    count = LV * LW
+    total = both[0:rows, 0:count] + (both[0:rows, count : 2 * count] + both[rows : 2 * rows, 0:count])
     for a in range(LU):
         for k in range(3):
             out_ref[k, :, pl.ds(LV * LW * a, LV * LW)] = total[3 * a + k : 3 * a + k + 1, :]
@@ -586,17 +593,24 @@
     return [pltpu.with_memory_space_constraint(array, pltpu.VMEM) for array in arrays]
 
 
-def volume_call(u, lam, disp, even, odd):
+def distant(*arrays):
+    return [pltpu.with_memory_space_constraint(array, pltpu.HBM) for array in arrays]
+
+
+def volume_call(u, lam, disp, even, odd, blk, coords, nb, cap):
     return pl.pallas_call(
-        volume_kernel,
-        in_specs=[HBM, HBM, VMEM, VMEM, VMEM],
-        out_specs=[HBM, VMEM, VMEM, VMEM, VMEM],
+        functools.partial(volume_kernel, nb, cap),
+        in_specs=[HBM, HBM] + [VMEM] * 5,
+        out_specs=[HBM] + [VMEM] * 7,
         out_shape=[
             jax.ShapeDtypeStruct((5, 64) + TILE, F32),
             pltpu.VMEM((2, 5, 16) + TILE, F32),
             pltpu.VMEM((2, 5, 16) + TILE, F32),
+            pltpu.VMEM((2, 5, 16) + TILE, F32),
             pltpu.VMEM((2, 2, 4, 3) + TILE, F32),
             pltpu.VMEM((2, 3, 2) + TILE, F32),
+            pltpu.VMEM((16, 128), F32),
+            pltpu.VMEM((3 * nb, 128), F32),
         ],
         scratch_shapes=[
             pltpu.VMEM((5, 64) + TILE, F32),
@@ -608,10 +622,13 @@
             pltpu.VMEM((4, 16, 5) + TILE, F32),
             pltpu.VMEM((16, 5) + TILE, F32),
             pltpu.VMEM((2, 4, 5) + TILE, F32),
-            pltpu.SemaphoreType.DMA((11,)),
+            pltpu.VMEM((9 * nb, 1024), jnp.bfloat16),
+            pltpu.VMEM((128, 1024), jnp.bfloat16),
+            pltpu.SemaphoreType.DMA((13,)),
         ],
+        compiler_params=pltpu.CompilerParams(vmem_limit_bytes=20 * 1024 * 1024),
         name="volume",
-    )(u, lam, *near(disp, even, odd))
+    )(*distant(u, lam), *near(disp, even, odd, blk, coords))
 
 
 def trace_call(lam, cube, blk, coords, disp):
@@ -633,74 +650,34 @@
             pltpu.VMEM(TILE, jnp.int32),
             pltpu.SemaphoreType.DMA((7,)),
         ],
+        compiler_params=pltpu.CompilerParams(vmem_limit_bytes=8 * 1024 * 1024),
         name="traces",
-    )(lam, cube, blk, coords, disp)
-
-
-def first_face_call(grad, u, own, received, gkeep, cols, g):
-    return pl.pallas_call(
-        first_face_kernel,
-        in_specs=[HBM] + [VMEM] * 6,
-        out_specs=[HBM, VMEM, VMEM],
-        out_shape=[
-            jax.ShapeDtypeStruct((5, 64) + TILE, F32),
-            pltpu.VMEM((2, 3) + TILE, F32),
-            pltpu.VMEM((6, 128), F32),
-        ],
-        scratch_shapes=[pltpu.VMEM((5, 16) + TILE, F32), pltpu.SemaphoreType.DMA((4,))],
-        input_output_aliases={0: 0},
-        name="faces_first",
-    )(grad, *near(u, own, received, gkeep, cols, g))
-
-
-def label_call(even, odd, far, rows, nb):
-    return pl.pallas_call(
-        functools.partial(label_kernel, nb),
-        in_specs=[VMEM] * 4,
-        out_specs=VMEM,
-        out_shape=pltpu.VMEM((32, 128), F32),
-        name="labels",
-    )(*near(even, odd, far, rows))
-
-
-def second_face_call(grad, u, own, received, gkeep, cols, g, part, rows, mine, labels, cpack, nb, cap, px):
+    )(*distant(lam, cube, blk, coords, disp))
+
+
+def face_call(even_recv, odd_recv, grad, *rest, nb, cap, px):
     height = -(-15 * cap // 128)
     return pl.pallas_call(
-        functools.partial(second_face_kernel, nb, cap, px),
-        in_specs=[HBM] + [VMEM] * 11,
+        functools.partial(face_kernel, nb, cap, px),
+        in_specs=[VMEM, VMEM, HBM] + [VMEM] * 10,
         out_specs=[HBM, VMEM, VMEM, VMEM],
         out_shape=[
             jax.ShapeDtypeStruct((5, 64) + TILE, F32),
-            pltpu.VMEM((nb * height, 128), F32),
+            jax.ShapeDtypeStruct((nb * height, 128), F32),
             pltpu.VMEM((2, 3) + TILE, F32),
             pltpu.VMEM((6, 128), F32),
         ],
         scratch_shapes=[
-            pltpu.VMEM((5, 16) + TILE, F32),
+            pltpu.VMEM((2, 5, 16) + TILE, F32),
+            pltpu.VMEM((32, 128), F32),
             pltpu.VMEM((6 * nb, 1024), jnp.bfloat16),
             pltpu.VMEM((128, 1024), jnp.bfloat16),
-            pltpu.SemaphoreType.DMA((4,)),
+            pltpu.SemaphoreType.DMA((2, 4)),
         ],
-        input_output_aliases={0: 0},
-        name="faces_second",
-    )(grad, *near(u, own, received, gkeep, cols, g, part, rows, mine, labels, cpack))
-
-
-def slot_call(blk, coords, nb, cap):
-    return pl.pallas_call(
-        functools.partial(slot_kernel, nb, cap),
-        in_specs=[VMEM, VMEM],
-        out_specs=[VMEM, VMEM],
-        out_shape=[
-            pltpu.VMEM((16, 128), F32),
-            pltpu.VMEM((3 * nb, 128), F32),
-        ],
-        scratch_shapes=[
-            pltpu.VMEM((9 * nb, 1024), jnp.bfloat16),
-            pltpu.VMEM((128, 1024), jnp.bfloat16),
-        ],
-        name="slots",
-    )(*near(blk, coords))
+        input_output_aliases={2: 0},
+        compiler_params=pltpu.CompilerParams(vmem_limit_bytes=12 * 1024 * 1024),
+        name="faces",
+    )(*near(even_recv, odd_recv), *distant(grad), *near(*rest))
 
 
 def lattice_call(buf, part, yrow, xrow, nb, cap, py):
@@ -712,9 +689,10 @@
             jax.ShapeDtypeStruct((3, 1, LU * LV * LW), F32),
         ],
         scratch_shapes=[
-            pltpu.VMEM((16 * 3 * LU, 128), F32),
+            pltpu.VMEM((16 * (3 * LU + 4), 128), F32),
             pltpu.VMEM((16 * LV * LW, 128), F32),
         ],
+        compiler_params=pltpu.CompilerParams(vmem_limit_bytes=8 * 1024 * 1024),
         name="lattice",
     )(*near(buf, part, yrow, xrow))
 
@@ -759,14 +737,11 @@
     second = swap(own_odd, "px", 1, False)
     even = swap(y_even, "py", 0, True)
     odd = swap(y_odd, "py", 1, True)
-    mine, cpack = slot_call(blk, coords, nb, cap)
     beside = jnp.where(lax.axis_index("py") % 2 == 0, even[80:81], odd[80:81])
     far = shift_px(jnp.concatenate([blk, beside]), -1)
-    grad, ukeep, gkeep, cols, g = volume_call(u, lam, disp, even, odd)
-    grad, part, rows = first_face_call(grad, ukeep, own_even, first, gkeep, cols, g)
-    labels = label_call(even, odd, far, rows, nb)
-    grad, buf, part, rows = second_face_call(
-        grad, ukeep, own_odd, second, gkeep, cols, g, part, rows, mine, labels, cpack, nb, cap, px
+    grad, lkeep, ukeep, gkeep, cols, g, mine, cpack = volume_call(u, lam, disp, even, odd, blk, coords, nb, cap)
+    grad, buf, part, rows = face_call(
+        first, second, grad, lkeep, ukeep, gkeep, cols, g, mine, even, odd, far, cpack, nb=nb, cap=cap, px=px
     )
     received = lax.all_to_all(buf, ("px", "py"), split_axis=0, concat_axis=0, tiled=True)
     yrow = shift_py(rows, 1)

time: 40 us -> 38 us (0.950)
  Pallas kernels: 12.4 us -> 10.1 us
  waiting for transfers between devices: 10.1 us -> 11.2 us
  starting transfers between devices: 16.2 us -> 15.6 us
    pallas_call x5 -> x2, Pallas kernels: 9.59 us -> 7.51 us  [the longest x1 5.39 us: volume_call(): pl.pallas_call(functools.partial(volume_kernel, nb, cap), in_specs=[HBM,...]
    ppermute x2, waiting for transfers between devices: 1.39 us -> 2.49 us  [shift_px(): return lax.ppermute(payload, 'px', pairs)]
    ppermute x4, starting transfers between devices: 6.03 us -> 5.32 us  [swap(): return lax.ppermute(payload, axis, pairs)]
  transfers between devices with their start and end apart: 8 -> 8, of which waited for: 4 -> 5; matrix products, arithmetic and copies ran while one was open for 0% -> 0% of each run, Pallas kernels for 18% -> 14%
where the time goes in v3:
time: 38 us; the launch traced here: 37.7 us
  starting transfers between devices  15.6 us (41%)
  waiting for transfers between devices  11.2 us (29%)
  Pallas kernels  10.1 us (27%)
  between operations  0.73 us (2%)
    ppermute x4, waiting for transfers between devices, swap(): return lax.ppermute(payload, axis, pairs)  5.87 us
    pallas_call x1, Pallas kernels, volume_call(): pl.pallas_call(functools.partial(volume_kernel, nb, cap), in_specs=[HBM,...  5.39 us
    ppermute x4, starting transfers between devices, swap(): return lax.ppermute(payload, axis, pairs)  5.32 us
    all_to_all x1, starting transfers between devices, per_device(): lax.all_to_all(buf, ('px', 'py'), split_axis=0, concat_axis=0, tiled=True)  5 us
    ppermute x2, starting transfers between devices, shift_px(): return lax.ppermute(payload, 'px', pairs)  4.96 us
    ppermute x1, waiting for transfers between devices, shift_py(): lax.ppermute(payload, 'py', [(i, (i + step) % length) for i in range(leng...  2.78 us
    ppermute x2, waiting for transfers between devices, shift_px(): return lax.ppermute(payload, 'px', pairs)  2.49 us
    pallas_call x1, Pallas kernels, face_call(): pl.pallas_call(functools.partial(face_kernel, nb, cap, px), in_specs=[VME...  2.12 us
  transfers between devices with their start and end apart: 8, of which 5 were waited for; matrix products, arithmetic and copies ran while one was open for 0% of the time, Pallas kernels for 14%

profile of v3, /device:TPU:0, one launch (start us, length us, event | category | flops | bytes accessed | tf_op | source)
XLA Modules:
  0.0 37.7 jit_solution(6440829961837274563)
XLA Ops:
  0.6 1.2 %traces.1 = (f32[5,16,8,128]{3,2,1,0:T(8,128)S(1)}, f32[5,16,8,128]{3,2,1,0:T(8,128)S(1)}, f32[81,128]{1,0:T(8,128)S(1)}, f32[81,128]{1,0:T(8,128)S(1)}, f32[8,1...) custom-call(f32[5,64,8,128]{3,2,1,0:T(8,128)} %bitcast.22, f32[5,4,4,4,8,128]{5,4,3,2,1,0:T(8,128)} %bitcast.23, ...), custom_call_target="tpu_custom_call" | custom-call | tf_op jit(solution)/shard_map/traces/pallas_call | solution.py:635
  1.8 0.5 %collective-permute-start.2 = (f32[81,128]{1,0:T(8,128)S(1)}, f32[81,128]{1,0:T(8,128)S(1)}, u32[]{:S(2)}, u32[]{:S(2)}) collective-permute-start(f32[81,128]{1,0:T(8,128)S(1)} %get-tuple-element.27), channel_id=1, source_target_pairs={{0,1},{1,0},{2,3},{3,2},{4,5},{5,4},{6,7},{7,6},{8,9},{9,8},{10,11... | collective-permute-start | bytes 124424 | tf_op jit(solution)/shard_map/ppermute | solution.py:718
  2.3 2.6 %collective-permute-start.3 = (f32[81,128]{1,0:T(8,128)S(1)}, f32[81,128]{1,0:T(8,128)S(1)}, u32[]{:S(2)}, u32[]{:S(2)}) collective-permute-start(f32[81,128]{1,0:T(8,128)S(1)} %get-tuple-element.28), channel_id=1, source_target_pairs={{1,2},{2,1},{3,0},{0,3},{5,6},{6,5},{7,4},{4,7},{9,10},{10,9},{11,... | collective-permute-start | bytes 124424 | tf_op jit(solution)/shard_map/ppermute | solution.py:718
  4.9 1.5 %collective-permute-start = (f32[5,16,8,128]{3,2,1,0:T(8,128)S(1)}, f32[5,16,8,128]{3,2,1,0:T(8,128)S(1)}, u32[]{:S(2)}, u32[]{:S(2)}) collective-permute-start(f32[5,16,8,128]{3,2,1,0:T(8,128)S(1)} %get-tuple-element.24), channel_id=1, source_target_pairs={{0,4},{4,0},{8,12},{12,8},{16,20},{20,16},{24,28},{28,24},{1,5},{5... | collective-permute-start | bytes 983048 | tf_op jit(solution)/shard_map/ppermute | solution.py:718
  6.5 0.7 %collective-permute-start.1 = (f32[5,16,8,128]{3,2,1,0:T(8,128)S(1)}, f32[5,16,8,128]{3,2,1,0:T(8,128)S(1)}, u32[]{:S(2)}, u32[]{:S(2)}) collective-permute-start(f32[5,16,8,128]{3,2,1,0:T(8,128)S(1)} %get-tuple-element.25), channel_id=1, source_target_pairs={{4,8},{8,4},{12,16},{16,12},{20,24},{24,20},{5,9},{9,5},{13,17},{1... | collective-permute-start | bytes 983048 | tf_op jit(solution)/shard_map/ppermute | solution.py:718
  7.1 0.0 collective-permute-done.2.even_ref
  7.1 0.0 collective-permute-done.3.odd_ref
  7.2 1.3 %collective-permute-start.4 = (f32[9,128]{1,0:T(8,128)S(1)}, f32[9,128]{1,0:T(8,128)S(1)}, u32[]{:S(2)}, u32[]{:S(2)}) collective-permute-start(f32[9,128]{1,0:T(8,128)S(1)} %pad_maximum_fusion), channel_id=1, source_target_pairs={{4,0},{8,4},{12,8},{16,12},{20,16},{24,20},{28,24},{5,1},{9,5},{13... | collective-permute-start | bytes 13832 | tf_op jit(solution)/shard_map/ppermute | solution.py:703
  8.5 5.4 %volume.1 = (f32[5,64,8,128]{3,2,1,0:T(8,128)}, f32[2,5,16,8,128]{4,3,2,1,0:T(8,128)S(1)}, f32[2,5,16,8,128]{4,3,2,1,0:T(8,128)S(1)}, f32[2,5,16,8,128]{4,3,2,1,...) custom-call(f32[5,64,8,128]{3,2,1,0:T(8,128)} %bitcast.25, ...), custom_call_target="tpu_custom_call" | custom-call | tf_op jit(solution)/shard_map/volume/pallas_call | solution.py:601
  13.9 1.1 %collective-permute-done.4.far_ref = f32[9,128]{1,0:T(8,128)S(1)} collective-permute-done((f32[9,128]{1,0:T(8,128)S(1)}, f32[9,128]{1,0:T(8,128)S(1)}, u32[]{:S(2)}, u32[]{:S(2)}) %collective-permute-start.4) | collective-permute-done | bytes 4640 | tf_op jit(solution)/shard_map/ppermute | solution.py:703
  15.0 5.9 %collective-permute-done.even_recv = f32[5,16,8,128]{3,2,1,0:T(8,128)S(1)} collective-permute-done((f32[5,16,8,128]{3,2,1,0:T(8,128)S(1)}, f32[5,16,8,128]{3,2,1,0:T(8,128)S(1)}, u32[]{:S(2)}, u32[]{:S(2)}) %collective-permute-start) | collective-permute-done | bytes 327712 | tf_op jit(solution)/shard_map/ppermute | solution.py:718
  20.8 0.0 collective-permute-done.1.odd_recv
  20.9 2.1 %faces.1 = (f32[5,64,8,128]{3,2,1,0:T(8,128)}, f32[256,128]{1,0:T(8,128)}, f32[2,3,8,128]{3,2,1,0:T(8,128)S(1)}, f32[6,128]{1,0:T(8,128)S(1)}) custom-call(f32[5,16,8,128]{3,2,1,0:T(8,128)S(1)} %collective-permute-done.even_recv, f32[5,16,8,128]{3,2,1,0:T(8,128)S(1)} %collective-permute-done.1.odd_recv, ...), custom_call_target="tpu_custom_call", output_to_operand_aliasing={{0}: (2, {})} | custom-call | tf_op jit(solution)/shard_map/faces/pallas_call | solution.py:660
  23.0 5.0 %all-to-all-start = ((f32[32,8,128]{2,1,0:T(8,128)}), f32[32,8,128]{2,1,0:T(8,128)S(1)}, u32[]{:S(2)}, u32[]{:S(2)}) async-start(f32[32,8,128]{2,1,0:T(8,128)} %bitcast.9), calls=%async_computation | async-start | bytes 262144 | tf_op jit(solution)/shard_map/all_to_all | solution.py:746
  28.0 0.3 collective-permute-start.5
  28.3 2.8 %collective-permute-done.5.yrow_ref = f32[6,128]{1,0:T(8,128)S(1)} collective-permute-done((f32[6,128]{1,0:T(8,128)S(1)}, f32[6,128]{1,0:T(8,128)S(1)}, u32[]{:S(2)}, u32[]{:S(2)}) %collective-permute-start.5) | collective-permute-done | bytes 3104 | tf_op jit(solution)/shard_map/ppermute | solution.py:708
  31.1 3.7 %collective-permute-start.6 = (f32[3,8,128]{2,1,0:T(8,128)S(1)}, f32[3,8,128]{2,1,0:T(8,128)S(1)}, u32[]{:S(2)}, u32[]{:S(2)}) collective-permute-start(f32[3,8,128]{2,1,0:T(8,128)S(1)} %bitcast_add_fusion), channel_id=1, source_target_pairs={{0,4},{4,8},{8,12},{12,16},{16,20},{20,24},{24,28},{1,5},{5,9},{9,... | collective-permute-start | bytes 36872 | tf_op jit(solution)/shard_map/ppermute | solution.py:703
  34.8 1.4 %collective-permute-done.6.xrow_ref = f32[3,8,128]{2,1,0:T(8,128)S(1)} collective-permute-done((f32[3,8,128]{2,1,0:T(8,128)S(1)}, f32[3,8,128]{2,1,0:T(8,128)S(1)}, u32[]{:S(2)}, u32[]{:S(2)}) %collective-permute-start.6) | collective-permute-done | bytes 12320 | tf_op jit(solution)/shard_map/ppermute | solution.py:703
  36.2 0.1 all-to-all-done
  36.2 1.5 %lattice.1 = (f32[3,8,128]{2,1,0:T(8,128)}, f32[3,1,864]{2,1,0:T(1,128)}) custom-call(f32[256,128]{1,0:T(8,128)S(1)} %bitcast.21, f32[2,3,8,128]{3,2,1,0:T(8,128)S(1)} %get-tuple-element.41.part_ref, f32[6,128]{1,0:T(8,128)S(1)} %collective-permute-done.5.yrow_ref, f32[3,8,128]{2,1,0:T(8,128)S(1)} %collective-permute-done.6.xrow_ref), custom_call_target="tpu_custom_call" | custom-call | tf_op jit(solution)/shard_map/lattice/pallas_call | solution.py:684
  (5 shorter events, 0.0 us)
Async XLA Ops:
  1.8 5.3 %collective-permute-start.2 = (f32[81,128]{1,0:T(8,128)S(1)}, f32[81,128]{1,0:T(8,128)S(1)}, u32[]{:S(2)}, u32[]{:S(2)}) collective-permute-start(f32[81,128]{1,0:T(8,128)S(1)} %get-tuple-element.27), channel_id=1, source_target_pairs={{0,1},{1,0},{2,3},{3,2},{4,5},{5,4},{6,7},{7,6},{8,9},{9,8},{10,11... | collective-permute-start | bytes 124424 | tf_op jit(solution)/shard_map/ppermute | solution.py:718
  2.3 4.8 %collective-permute-start.3 = (f32[81,128]{1,0:T(8,128)S(1)}, f32[81,128]{1,0:T(8,128)S(1)}, u32[]{:S(2)}, u32[]{:S(2)}) collective-permute-start(f32[81,128]{1,0:T(8,128)S(1)} %get-tuple-element.28), channel_id=1, source_target_pairs={{1,2},{2,1},{3,0},{0,3},{5,6},{6,5},{7,4},{4,7},{9,10},{10,9},{11,... | collective-permute-start | bytes 124424 | tf_op jit(solution)/shard_map/ppermute | solution.py:718
  4.9 15.9 %collective-permute-start = (f32[5,16,8,128]{3,2,1,0:T(8,128)S(1)}, f32[5,16,8,128]{3,2,1,0:T(8,128)S(1)}, u32[]{:S(2)}, u32[]{:S(2)}) collective-permute-start(f32[5,16,8,128]{3,2,1,0:T(8,128)S(1)} %get-tuple-element.24), channel_id=1, source_target_pairs={{0,4},{4,0},{8,12},{12,8},{16,20},{20,16},{24,28},{28,24},{1,5},{5... | collective-permute-start | bytes 983048 | tf_op jit(solution)/shard_map/ppermute | solution.py:718
  6.5 14.4 %collective-permute-start.1 = (f32[5,16,8,128]{3,2,1,0:T(8,128)S(1)}, f32[5,16,8,128]{3,2,1,0:T(8,128)S(1)}, u32[]{:S(2)}, u32[]{:S(2)}) collective-permute-start(f32[5,16,8,128]{3,2,1,0:T(8,128)S(1)} %get-tuple-element.25), channel_id=1, source_target_pairs={{4,8},{8,4},{12,16},{16,12},{20,24},{24,20},{5,9},{9,5},{13,17},{1... | collective-permute-start | bytes 983048 | tf_op jit(solution)/shard_map/ppermute | solution.py:718
  7.2 7.8 %collective-permute-start.4 = (f32[9,128]{1,0:T(8,128)S(1)}, f32[9,128]{1,0:T(8,128)S(1)}, u32[]{:S(2)}, u32[]{:S(2)}) collective-permute-start(f32[9,128]{1,0:T(8,128)S(1)} %pad_maximum_fusion), channel_id=1, source_target_pairs={{4,0},{8,4},{12,8},{16,12},{20,16},{24,20},{28,24},{5,1},{9,5},{13... | collective-permute-start | bytes 13832 | tf_op jit(solution)/shard_map/ppermute | solution.py:703
  23.0 13.2 %all-to-all-start = ((f32[32,8,128]{2,1,0:T(8,128)}), f32[32,8,128]{2,1,0:T(8,128)S(1)}, u32[]{:S(2)}, u32[]{:S(2)}) async-start(f32[32,8,128]{2,1,0:T(8,128)} %bitcast.9), calls=%async_computation | async-start | bytes 262144 | tf_op jit(solution)/shard_map/all_to_all | solution.py:746
  28.0 3.1 %collective-permute-start.5 = (f32[6,128]{1,0:T(8,128)S(1)}, f32[6,128]{1,0:T(8,128)S(1)}, u32[]{:S(2)}, u32[]{:S(2)}) collective-permute-start(f32[6,128]{1,0:T(8,128)S(1)} %get-tuple-element.42), channel_id=1, source_target_pairs={{0,1},{1,2},{2,3},{3,0},{4,5},{5,6},{6,7},{7,4},{8,9},{9,10},{10,1... | collective-permute-start | bytes 9224 | tf_op jit(solution)/shard_map/ppermute | solution.py:708
  31.1 5.1 %collective-permute-start.6 = (f32[3,8,128]{2,1,0:T(8,128)S(1)}, f32[3,8,128]{2,1,0:T(8,128)S(1)}, u32[]{:S(2)}, u32[]{:S(2)}) collective-permute-start(f32[3,8,128]{2,1,0:T(8,128)S(1)} %bitcast_add_fusion), channel_id=1, source_target_pairs={{0,4},{4,8},{8,12},{12,16},{16,20},{20,24},{24,28},{1,5},{5,9},{9,... | collective-permute-start | bytes 36872 | tf_op jit(solution)/shard_map/ppermute | solution.py:703

commit v4 on v3

--- a/solution.py
+++ b/solution.py
@@ -168,7 +168,7 @@
     for copy in copies[2:5]:
         copy.wait()
     blkf[...] = blocks[...].astype(F32)
-    rows = tiles.reshape(1280, 128)
+    rows = tiles.reshape(1920, 128)
     bottom = rows[pl.ds(0, 80, stride=8), :]
     top = rows[pl.ds(640 + 7, 80, stride=8), :]
     y_even[0:80, :] = jnp.where(y_up == 1, top, bottom)
@@ -527,7 +527,7 @@
     rows = lax.broadcasted_iota(jnp.int32, TILE, 0)
     for k in range(3):
         beside = jnp.broadcast_to(yrow_ref[k : k + 1, :], TILE)
-        owned_ref[k] = part_ref[0, k] + jnp.where(rows == 0, beside, 0.0) + xrow_ref[k]
+        owned_ref[k] = part_ref[0, k] + jnp.where(rows == 0, beside, 0.0) + xrow_ref[pl.ds(8 * k, 8), :]
     per_row = 128 // cap
     height = buf_ref.shape[0] // nb
     source = lax.broadcasted_iota(jnp.int32, (nb, 128), 0)
@@ -646,7 +646,7 @@
             pltpu.VMEM((27, 2, 128), F32),
         ],
         scratch_shapes=[
-            pltpu.VMEM((2, 5, 4, 4) + TILE, F32),
+            pltpu.VMEM((3, 5, 4, 4) + TILE, F32),
             pltpu.VMEM(TILE, jnp.int32),
             pltpu.SemaphoreType.DMA((7,)),
         ],
@@ -689,8 +689,8 @@
             jax.ShapeDtypeStruct((3, 1, LU * LV * LW), F32),
         ],
         scratch_shapes=[
-            pltpu.VMEM((16 * (3 * LU + 4), 128), F32),
-            pltpu.VMEM((16 * LV * LW, 128), F32),
+            pltpu.VMEM((16 * (3 * LU + 5), 128), F32),
+            pltpu.VMEM((16 * (LV * LW + 1), 128), F32),
         ],
         compiler_params=pltpu.CompilerParams(vmem_limit_bytes=8 * 1024 * 1024),
         name="lattice",
@@ -744,9 +744,8 @@
         first, second, grad, lkeep, ukeep, gkeep, cols, g, mine, even, odd, far, cpack, nb=nb, cap=cap, px=px
     )
     received = lax.all_to_all(buf, ("px", "py"), split_axis=0, concat_axis=0, tiled=True)
-    yrow = shift_py(rows, 1)
-    below = jnp.pad(yrow[3:6, None, :], ((0, 0), (0, 7), (0, 0)))
-    xrow = shift_px(part[1] + below, 1)
+    xrow = shift_px(jnp.concatenate([part[1].reshape(24, 128), rows[3:6]]), 1)
+    yrow = shift_py(rows[0:3] + xrow[24:27], 1)
     owned, lattice = lattice_call(received, part, yrow, xrow, nb, cap, py)
     return (
         grad.reshape(5, 64, 1, 8, 128),

time: 38 us -> 38 us (level)
  no operation moved by 1% of the time
where the time goes in v4:
time: 38 us; the launch traced here: 37.7 us
  starting transfers between devices  15.3 us (40%)
  waiting for transfers between devices  11.5 us (30%)
  Pallas kernels  10.1 us (27%)
  between operations  0.76 us (2%)
    ppermute x4, waiting for transfers between devices, swap(): return lax.ppermute(payload, axis, pairs)  5.87 us
    pallas_call x1, Pallas kernels, volume_call(): pl.pallas_call(functools.partial(volume_kernel, nb, cap), in_specs=[HBM,...  5.39 us
    ppermute x4, starting transfers between devices, swap(): return lax.ppermute(payload, axis, pairs)  5.32 us
    all_to_all x1, starting transfers between devices, per_device(): lax.all_to_all(buf, ('px', 'py'), split_axis=0, concat_axis=0, tiled=True)  5 us
    ppermute x2, starting transfers between devices, shift_px(): return lax.ppermute(payload, 'px', pairs)  4.97 us
    ppermute x1, waiting for transfers between devices, shift_py(): lax.ppermute(payload, 'py', [(i, (i + step) % length) for i in range(leng...  3.01 us
    ppermute x2, waiting for transfers between devices, shift_px(): return lax.ppermute(payload, 'px', pairs)  2.53 us
    pallas_call x1, Pallas kernels, face_call(): pl.pallas_call(functools.partial(face_kernel, nb, cap, px), in_specs=[VME...  2.12 us
  transfers between devices with their start and end apart: 8, of which 5 were waited for; matrix products, arithmetic and copies ran while one was open for 0% of the time, Pallas kernels for 14%

profile of v4, /device:TPU:0, one launch (start us, length us, event | category | flops | bytes accessed | tf_op | source)
XLA Modules:
  0.0 37.7 jit_solution(11518377464772037)
XLA Ops:
  0.6 1.2 %traces.1 = (f32[5,16,8,128]{3,2,1,0:T(8,128)S(1)}, f32[5,16,8,128]{3,2,1,0:T(8,128)S(1)}, f32[81,128]{1,0:T(8,128)S(1)}, f32[81,128]{1,0:T(8,128)S(1)}, f32[8,1...) custom-call(f32[5,64,8,128]{3,2,1,0:T(8,128)} %bitcast.22, f32[5,4,4,4,8,128]{5,4,3,2,1,0:T(8,128)} %bitcast.23, ...), custom_call_target="tpu_custom_call" | custom-call | tf_op jit(solution)/shard_map/traces/pallas_call | solution.py:635
  1.8 0.5 %collective-permute-start.2 = (f32[81,128]{1,0:T(8,128)S(1)}, f32[81,128]{1,0:T(8,128)S(1)}, u32[]{:S(2)}, u32[]{:S(2)}) collective-permute-start(f32[81,128]{1,0:T(8,128)S(1)} %get-tuple-element.27), channel_id=1, source_target_pairs={{0,1},{1,0},{2,3},{3,2},{4,5},{5,4},{6,7},{7,6},{8,9},{9,8},{10,11... | collective-permute-start | bytes 124424 | tf_op jit(solution)/shard_map/ppermute | solution.py:718
  2.3 2.6 %collective-permute-start.3 = (f32[81,128]{1,0:T(8,128)S(1)}, f32[81,128]{1,0:T(8,128)S(1)}, u32[]{:S(2)}, u32[]{:S(2)}) collective-permute-start(f32[81,128]{1,0:T(8,128)S(1)} %get-tuple-element.28), channel_id=1, source_target_pairs={{1,2},{2,1},{3,0},{0,3},{5,6},{6,5},{7,4},{4,7},{9,10},{10,9},{11,... | collective-permute-start | bytes 124424 | tf_op jit(solution)/shard_map/ppermute | solution.py:718
  4.9 1.5 %collective-permute-start = (f32[5,16,8,128]{3,2,1,0:T(8,128)S(1)}, f32[5,16,8,128]{3,2,1,0:T(8,128)S(1)}, u32[]{:S(2)}, u32[]{:S(2)}) collective-permute-start(f32[5,16,8,128]{3,2,1,0:T(8,128)S(1)} %get-tuple-element.24), channel_id=1, source_target_pairs={{0,4},{4,0},{8,12},{12,8},{16,20},{20,16},{24,28},{28,24},{1,5},{5... | collective-permute-start | bytes 983048 | tf_op jit(solution)/shard_map/ppermute | solution.py:718
  6.5 0.7 %collective-permute-start.1 = (f32[5,16,8,128]{3,2,1,0:T(8,128)S(1)}, f32[5,16,8,128]{3,2,1,0:T(8,128)S(1)}, u32[]{:S(2)}, u32[]{:S(2)}) collective-permute-start(f32[5,16,8,128]{3,2,1,0:T(8,128)S(1)} %get-tuple-element.25), channel_id=1, source_target_pairs={{4,8},{8,4},{12,16},{16,12},{20,24},{24,20},{5,9},{9,5},{13,17},{1... | collective-permute-start | bytes 983048 | tf_op jit(solution)/shard_map/ppermute | solution.py:718
  7.1 0.0 collective-permute-done.2.even_ref
  7.1 0.0 collective-permute-done.3.odd_ref
  7.2 1.3 %collective-permute-start.4 = (f32[9,128]{1,0:T(8,128)S(1)}, f32[9,128]{1,0:T(8,128)S(1)}, u32[]{:S(2)}, u32[]{:S(2)}) collective-permute-start(f32[9,128]{1,0:T(8,128)S(1)} %pad_maximum_fusion.1), channel_id=1, source_target_pairs={{4,0},{8,4},{12,8},{16,12},{20,16},{24,20},{28,24},{5,1},{9,5},{13... | collective-permute-start | bytes 13832 | tf_op jit(solution)/shard_map/ppermute | solution.py:703
  8.5 5.4 %volume.1 = (f32[5,64,8,128]{3,2,1,0:T(8,128)}, f32[2,5,16,8,128]{4,3,2,1,0:T(8,128)S(1)}, f32[2,5,16,8,128]{4,3,2,1,0:T(8,128)S(1)}, f32[2,5,16,8,128]{4,3,2,1,...) custom-call(f32[5,64,8,128]{3,2,1,0:T(8,128)} %bitcast.25, ...), custom_call_target="tpu_custom_call" | custom-call | tf_op jit(solution)/shard_map/volume/pallas_call | solution.py:601
  13.9 1.1 %collective-permute-done.4.far_ref = f32[9,128]{1,0:T(8,128)S(1)} collective-permute-done((f32[9,128]{1,0:T(8,128)S(1)}, f32[9,128]{1,0:T(8,128)S(1)}, u32[]{:S(2)}, u32[]{:S(2)}) %collective-permute-start.4) | collective-permute-done | bytes 4640 | tf_op jit(solution)/shard_map/ppermute | solution.py:703
  15.0 5.9 %collective-permute-done.even_recv = f32[5,16,8,128]{3,2,1,0:T(8,128)S(1)} collective-permute-done((f32[5,16,8,128]{3,2,1,0:T(8,128)S(1)}, f32[5,16,8,128]{3,2,1,0:T(8,128)S(1)}, u32[]{:S(2)}, u32[]{:S(2)}) %collective-permute-start) | collective-permute-done | bytes 327712 | tf_op jit(solution)/shard_map/ppermute | solution.py:718
  20.8 0.0 collective-permute-done.1.odd_recv
  20.9 2.1 %faces.1 = (f32[5,64,8,128]{3,2,1,0:T(8,128)}, f32[256,128]{1,0:T(8,128)}, f32[2,3,8,128]{3,2,1,0:T(8,128)S(1)}, f32[6,128]{1,0:T(8,128)S(1)}) custom-call(f32[5,16,8,128]{3,2,1,0:T(8,128)S(1)} %collective-permute-done.even_recv, f32[5,16,8,128]{3,2,1,0:T(8,128)S(1)} %collective-permute-done.1.odd_recv, ...), custom_call_target="tpu_custom_call", output_to_operand_aliasing={{0}: (2, {})} | custom-call | tf_op jit(solution)/shard_map/faces/pallas_call | solution.py:660
  23.0 5.0 %all-to-all-start = ((f32[32,8,128]{2,1,0:T(8,128)}), f32[32,8,128]{2,1,0:T(8,128)S(1)}, u32[]{:S(2)}, u32[]{:S(2)}) async-start(f32[32,8,128]{2,1,0:T(8,128)} %bitcast.9), calls=%async_computation | async-start | bytes 262144 | tf_op jit(solution)/shard_map/all_to_all | solution.py:746
  28.0 3.7 %collective-permute-start.5 = (f32[27,128]{1,0:T(8,128)S(1)}, f32[27,128]{1,0:T(8,128)S(1)}, u32[]{:S(2)}, u32[]{:S(2)}) collective-permute-start(f32[27,128]{1,0:T(8,128)S(1)} %pad_maximum_fusion), channel_id=1, source_target_pairs={{0,4},{4,8},{8,12},{12,16},{16,20},{20,24},{24,28},{1,5},{5,9},{9,... | collective-permute-start | bytes 41480 | tf_op jit(solution)/shard_map/ppermute | solution.py:703
  31.7 1.4 %collective-permute-done.5.xrow_ref = f32[27,128]{1,0:T(8,128)S(1)} collective-permute-done((f32[27,128]{1,0:T(8,128)S(1)}, f32[27,128]{1,0:T(8,128)S(1)}, u32[]{:S(2)}, u32[]{:S(2)}) %collective-permute-start.5) | collective-permute-done | bytes 13856 | tf_op jit(solution)/shard_map/ppermute | solution.py:703
  33.1 0.0 collective-permute-start.6
  33.1 3.0 %collective-permute-done.6.yrow_ref = f32[3,128]{1,0:T(4,128)S(1)} collective-permute-done((f32[3,128]{1,0:T(4,128)S(1)}, f32[3,128]{1,0:T(4,128)S(1)}, u32[]{:S(2)}, u32[]{:S(2)}) %collective-permute-start.6) | collective-permute-done | bytes 1568 | tf_op jit(solution)/shard_map/ppermute | solution.py:708
  36.1 0.1 all-to-all-done
  36.2 1.5 %lattice.1 = (f32[3,8,128]{2,1,0:T(8,128)}, f32[3,1,864]{2,1,0:T(1,128)}) custom-call(f32[256,128]{1,0:T(8,128)S(1)} %bitcast.21, f32[2,3,8,128]{3,2,1,0:T(8,128)S(1)} %get-tuple-element.41.part_ref, f32[3,128]{1,0:T(4,128)S(1)} %collective-permute-done.6.yrow_ref, f32[27,128]{1,0:T(8,128)S(1)} %collective-permute-done.5.xrow_ref), custom_call_target="tpu_custom_call" | custom-call | tf_op jit(solution)/shard_map/lattice/pallas_call | solution.py:684
  (6 shorter events, 0.0 us)
Async XLA Ops:
  1.8 5.3 %collective-permute-start.2 = (f32[81,128]{1,0:T(8,128)S(1)}, f32[81,128]{1,0:T(8,128)S(1)}, u32[]{:S(2)}, u32[]{:S(2)}) collective-permute-start(f32[81,128]{1,0:T(8,128)S(1)} %get-tuple-element.27), channel_id=1, source_target_pairs={{0,1},{1,0},{2,3},{3,2},{4,5},{5,4},{6,7},{7,6},{8,9},{9,8},{10,11... | collective-permute-start | bytes 124424 | tf_op jit(solution)/shard_map/ppermute | solution.py:718
  2.3 4.8 %collective-permute-start.3 = (f32[81,128]{1,0:T(8,128)S(1)}, f32[81,128]{1,0:T(8,128)S(1)}, u32[]{:S(2)}, u32[]{:S(2)}) collective-permute-start(f32[81,128]{1,0:T(8,128)S(1)} %get-tuple-element.28), channel_id=1, source_target_pairs={{1,2},{2,1},{3,0},{0,3},{5,6},{6,5},{7,4},{4,7},{9,10},{10,9},{11,... | collective-permute-start | bytes 124424 | tf_op jit(solution)/shard_map/ppermute | solution.py:718
  4.9 15.9 %collective-permute-start = (f32[5,16,8,128]{3,2,1,0:T(8,128)S(1)}, f32[5,16,8,128]{3,2,1,0:T(8,128)S(1)}, u32[]{:S(2)}, u32[]{:S(2)}) collective-permute-start(f32[5,16,8,128]{3,2,1,0:T(8,128)S(1)} %get-tuple-element.24), channel_id=1, source_target_pairs={{0,4},{4,0},{8,12},{12,8},{16,20},{20,16},{24,28},{28,24},{1,5},{5... | collective-permute-start | bytes 983048 | tf_op jit(solution)/shard_map/ppermute | solution.py:718
  6.5 14.4 %collective-permute-start.1 = (f32[5,16,8,128]{3,2,1,0:T(8,128)S(1)}, f32[5,16,8,128]{3,2,1,0:T(8,128)S(1)}, u32[]{:S(2)}, u32[]{:S(2)}) collective-permute-start(f32[5,16,8,128]{3,2,1,0:T(8,128)S(1)} %get-tuple-element.25), channel_id=1, source_target_pairs={{4,8},{8,4},{12,16},{16,12},{20,24},{24,20},{5,9},{9,5},{13,17},{1... | collective-permute-start | bytes 983048 | tf_op jit(solution)/shard_map/ppermute | solution.py:718
  7.2 7.8 %collective-permute-start.4 = (f32[9,128]{1,0:T(8,128)S(1)}, f32[9,128]{1,0:T(8,128)S(1)}, u32[]{:S(2)}, u32[]{:S(2)}) collective-permute-start(f32[9,128]{1,0:T(8,128)S(1)} %pad_maximum_fusion.1), channel_id=1, source_target_pairs={{4,0},{8,4},{12,8},{16,12},{20,16},{24,20},{28,24},{5,1},{9,5},{13... | collective-permute-start | bytes 13832 | tf_op jit(solution)/shard_map/ppermute | solution.py:703
  23.0 13.2 %all-to-all-start = ((f32[32,8,128]{2,1,0:T(8,128)}), f32[32,8,128]{2,1,0:T(8,128)S(1)}, u32[]{:S(2)}, u32[]{:S(2)}) async-start(f32[32,8,128]{2,1,0:T(8,128)} %bitcast.9), calls=%async_computation | async-start | bytes 262144 | tf_op jit(solution)/shard_map/all_to_all | solution.py:746
  28.0 5.1 %collective-permute-start.5 = (f32[27,128]{1,0:T(8,128)S(1)}, f32[27,128]{1,0:T(8,128)S(1)}, u32[]{:S(2)}, u32[]{:S(2)}) collective-permute-start(f32[27,128]{1,0:T(8,128)S(1)} %pad_maximum_fusion), channel_id=1, source_target_pairs={{0,4},{4,8},{8,12},{12,16},{16,20},{20,24},{24,28},{1,5},{5,9},{9,... | collective-permute-start | bytes 41480 | tf_op jit(solution)/shard_map/ppermute | solution.py:703
  33.1 3.0 %collective-permute-start.6 = (f32[3,128]{1,0:T(4,128)S(1)}, f32[3,128]{1,0:T(4,128)S(1)}, u32[]{:S(2)}, u32[]{:S(2)}) collective-permute-start(f32[3,128]{1,0:T(4,128)S(1)} %slice_add_fusion), channel_id=1, source_target_pairs={{0,1},{1,2},{2,3},{3,0},{4,5},{5,6},{6,7},{7,4},{8,9},{9,10},{10,1... | collective-permute-start | bytes 4616 | tf_op jit(solution)/shard_map/ppermute | solution.py:708
